TPU v7x, 256 devices: a whole 4x4x8 slice. The times are simulated.
256 devices in a mesh: lon: 32 (over y, z), lat: 8 (over x, core).
Axes of the slice: x: 4, y: 4, z: 8, core: 2. Of those that a mesh axis runs over, the one named last changes fastest.
Arguments:
- surface_adjoint: float32 [2048, 32768], P('lat', 'lon'), may hold values from -6 to 6
- east_adjoint: float32 [2048, 32768], P('lat', 'lon'), may hold values from -6 to 6
- north_adjoint: float32 [2048, 32768], P('lat', 'lon'), may hold values from -6 to 6
- water_depth: float32 [2048, 32768], P('lat', 'lon'), may hold values from 0.3 to 1
- wet_mask: int32 [2048, 32768], P('lat', 'lon'), may hold values 0 or 1
- control_active: int32 [128, 2048], P('lat', 'lon'), may hold values 0 or 1
Outputs:
- surface_after: float32 [2048, 32768], P('lat', 'lon')
- east_after: float32 [2048, 32768], P('lat', 'lon')
- north_after: float32 [2048, 32768], P('lat', 'lon')
- uplift_grad: float32 [128, 2048], P('lat', 'lon')
All inputs are finite; a program needn't handle non-finite values. No bound on the sum of `wet_mask` or of `control_active` on one device may be relied on, other than what follows from the above.
Results may differ from a plain program's by a relative error of at most 0.00021.
Values sent between devices are 32-bit elements; how exact they have to be, the bound alone decides.
A program may use at most 64 MiB of HBM per device.

v0:
```python
import jax
import jax.numpy as jnp
from jax import lax
from jax.sharding import PartitionSpec as P

SPACING = 16
STEPS = 3


courant = 0.5


def with_halo(array, sides, width):
    for axis, dim in sides:
        size, length = (lax.axis_size(axis), array.shape[dim])
        up = [(i, (i + 1) % size) for i in range(size - 1)]
        down = [(j, i) for i, j in up]
        last = lax.slice_in_dim(array, length - width, length, axis=dim)
        initial = lax.slice_in_dim(array, 0, width, axis=dim)
        before = lax.ppermute(last, axis, up)
        after = lax.ppermute(initial, axis, down)
        array = jnp.concatenate([before, array, after], axis=dim)
    return array


def spline_weight(arg):
    mag = jnp.abs(arg)
    inner = 2.0 / 3.0 - mag * mag + 0.5 * mag * mag * mag
    outer = (2.0 - mag) * (2.0 - mag) * (2.0 - mag) / 6.0
    return jnp.where(mag < 1.0, inner, jnp.where(mag < 2.0, outer, 0.0 * mag))


def spline_table(cells, points):
    rows = (jnp.arange(cells, dtype=jnp.float32)[:, None] + 0.5) / SPACING
    cols = jnp.arange(points + 4, dtype=jnp.float32)[None, :] - 2.0 + 0.5
    return spline_weight(rows - cols)


def fold_columns(extended):
    folded = extended[:, 4:-4]
    folded = folded.at[:, 0:2].add(extended[:, 0:2])
    folded = folded.at[:, -2:].add(extended[:, -2:])
    return folded


def fold_rows(extended):
    folded = extended[4:-4]
    folded = folded.at[0:2].add(extended[0:2])
    folded = folded.at[-2:].add(extended[-2:])
    return folded


def local(surface_adjoint, east_adjoint, north_adjoint, water_depth, wet_mask, control_active):
    wet_fraction = wet_mask.astype(jnp.float32)
    wet_depth = water_depth * wet_fraction
    surface_height, eastward, northward = (surface_adjoint, east_adjoint, north_adjoint)
    for step in range(STEPS):
        padded = with_halo(surface_height, (("lon", 1), ("lat", 0)), 1)
        eastward = wet_fraction * (
            eastward + courant * wet_depth * (padded[1:-1, 2:] - padded[1:-1, :-2])
        )
        northward = wet_fraction * (
            northward + courant * wet_depth * (padded[2:, 1:-1] - padded[:-2, 1:-1])
        )
        east_pad, north_padding = (
            with_halo(eastward, (("lon", 1), ("lat", 0)), 1),
            with_halo(northward, (("lon", 1), ("lat", 0)), 1),
        )
        surface_height = wet_fraction * (
            surface_height
            + courant
            * (
                east_pad[1:-1, 2:]
                - east_pad[1:-1, :-2]
                + (north_padding[2:, 1:-1] - north_padding[:-2, 1:-1])
            )
        )
    lat_cells, longitude_cells = surface_height.shape
    lat_points = lat_cells // SPACING
    lon_points = longitude_cells // SPACING
    lat_table = spline_table(lat_cells, lat_points)
    lon_table = spline_table(longitude_cells, lon_points)
    reduced = jnp.dot(
        lat_table.T,
        surface_height,
        precision=lax.Precision.HIGHEST,
        preferred_element_type=jnp.float32,
    )
    partial_value = jnp.dot(
        reduced, lon_table, precision=lax.Precision.HIGHEST, preferred_element_type=jnp.float32
    )
    extended = with_halo(partial_value, (("lon", 1), ("lat", 0)), 2)
    sums = fold_columns(fold_rows(extended))
    uplift_grad = sums * control_active.astype(jnp.float32) / SPACING
    return (surface_height, eastward, northward, uplift_grad)


def solution(mesh):
    return jax.shard_map(
        local,
        mesh=mesh,
        in_specs=(
            P("lat", "lon"),
            P("lat", "lon"),
            P("lat", "lon"),
            P("lat", "lon"),
            P("lat", "lon"),
            P("lat", "lon"),
        ),
        out_specs=(P("lat", "lon"), P("lat", "lon"), P("lat", "lon"), P("lat", "lon")),
        check_vma=False,
    )
```

profile of v0, /device:TPU:25, one launch (start us, length us, event | category | flops | bytes accessed | tf_op | source)
XLA Modules:
  0.0 200.3 jit_solution(8108705361946766711)
XLA Ops:
  1.7 7.7 %collective-permute-start = (f32[256,1]{1,0:T(8,128)S(1)}, f32[256,1]{1,0:T(8,128)S(1)}, u32[]{:S(2)}, u32[]{:S(2)}) collective-permute-start(f32[256,1]{1,0:T(8,128)S(1)} %get-tuple-element.86), channel_id=1, source_target_pairs={{8,0},{16,8},{24,16},{32,24},{40,32},{48,40},{56,48},{64,56},{72,6... | collective-permute-start | bytes 3080 | tf_op jit(solution)/shard_map/ppermute | solution.py:21
  11.5 5.8 %collective-permute-done.1 = f32[256,1]{1,0:T(8,128)S(1)} collective-permute-done((f32[256,1]{1,0:T(8,128)S(1)}, f32[256,1]{1,0:T(8,128)S(1)}, u32[]{:S(2)}, u32[]{:S(2)}) %collective-permute-start.1) | collective-permute-done | bytes 1056 | tf_op jit(solution)/shard_map/ppermute | solution.py:20
  20.5 4.0 %collective-permute-start.4 = (f32[1,1026]{1,0:T(1,128)S(1)}, f32[1,1026]{1,0:T(1,128)S(1)}, u32[]{:S(2)}, u32[]{:S(2)}) collective-permute-start(f32[1,1026]{1,0:T(1,128)S(1)} %get-tuple-element.68), channel_id=1, source_target_pairs={{1,0},{2,1},{3,2},{4,3},{5,4},{6,5},{7,6},{9,8},{10,9},{11,10},{12... | collective-permute-start | bytes 12320 | tf_op jit(solution)/shard_map/ppermute | solution.py:21
  28.3 4.8 %fusion.41 = (f32[256,1024]{1,0:T(8,128)}, f32[256,1024]{1,0:T(8,128)S(1)}) fusion(f32[256,1024]{1,0:T(8,128)} %param.15, f32[256,1024]{1,0:T(8,128)S(1)} %copy-done.1, f32[256,1]{1,0:T(8,128)S(1)} %collective-permute-done.1, f32[256,1]{1,0:T(8,128)S(1)} %collective-permute-done, s32[256,1024]{1,0:T(8,128)S(1)} %copy-done, f32[256,1024]{1,0:T(8,128)} %param.17, ...), kind=kLoop, calls=%fused_computation.64 | loop fusion | flops 3932160 | bytes 8400912 | tf_op jit(solution)/shard_map/mul | solution.py:59
  35.1 5.5 %collective-permute-start.7 = (f32[256,1]{1,0:T(8,128)S(1)}, f32[256,1]{1,0:T(8,128)S(1)}, u32[]{:S(2)}, u32[]{:S(2)}) collective-permute-start(f32[256,1]{1,0:T(8,128)S(1)} %get-tuple-element.84), channel_id=1, source_target_pairs={{8,0},{16,8},{24,16},{32,24},{40,32},{48,40},{56,48},{64,56},{72,6... | collective-permute-start | bytes 3080 | tf_op jit(solution)/shard_map/ppermute | solution.py:21
  48.4 3.6 %collective-permute-start.9 = (f32[1,1026]{1,0:T(1,128)S(1)}, f32[1,1026]{1,0:T(1,128)S(1)}, u32[]{:S(2)}, u32[]{:S(2)}) collective-permute-start(f32[1,1026]{1,0:T(1,128)S(1)} %get-tuple-element.67), channel_id=1, source_target_pairs={{0,1},{1,2},{2,3},{3,4},{4,5},{5,6},{6,7},{8,9},{9,10},{10,11},{11... | collective-permute-start | bytes 12320 | tf_op jit(solution)/shard_map/ppermute | solution.py:20
  53.0 6.2 %collective-permute-start.2 = (f32[256,1]{1,0:T(8,128)S(1)}, f32[256,1]{1,0:T(8,128)S(1)}, u32[]{:S(2)}, u32[]{:S(2)}) collective-permute-start(f32[256,1]{1,0:T(8,128)S(1)} %get-tuple-element.82), channel_id=1, source_target_pairs={{8,0},{16,8},{24,16},{32,24},{40,32},{48,40},{56,48},{64,56},{72,6... | collective-permute-start | bytes 3080 | tf_op jit(solution)/shard_map/ppermute | solution.py:21
  61.8 6.2 %collective-permute-done.3 = f32[256,1]{1,0:T(8,128)S(1)} collective-permute-done((f32[256,1]{1,0:T(8,128)S(1)}, f32[256,1]{1,0:T(8,128)S(1)}, u32[]{:S(2)}, u32[]{:S(2)}) %collective-permute-start.3) | collective-permute-done | bytes 1056 | tf_op jit(solution)/shard_map/ppermute | solution.py:20
  68.1 3.6 %fusion.32 = f32[256,1024]{1,0:T(8,128)S(1)} fusion(f32[256,1024]{1,0:T(8,128)S(1)} %copy-done.1, f32[256,1026]{1,0:T(8,128)} %concatenate.117, f32[1,1026]{1,0:T(1,128)S(1)} %collective-permute-done.9, f32[1,1026]{1,0:T(1,128)S(1)} %collective-permute-done.8, f32[256,1024]{1,0:T(8,128)} %get-tuple-element.56, f32[256,1]{1,0:T(8,128)S(1)} %collective-permute-done.3, ...), kind=kLoop, calls=%fused_computation.49 | loop fusion | flops 2883584 | bytes 5255184 | tf_op jit(solution)/shard_map/mul | solution.py:69
  78.3 4.0 %collective-permute-done.11 = f32[256,1]{1,0:T(8,128)S(1)} collective-permute-done((f32[256,1]{1,0:T(8,128)S(1)}, f32[256,1]{1,0:T(8,128)S(1)}, u32[]{:S(2)}, u32[]{:S(2)}) %collective-permute-start.11) | collective-permute-done | bytes 1056 | tf_op jit(solution)/shard_map/ppermute | solution.py:20
  87.7 3.5 %collective-permute-start.15 = (f32[1,1026]{1,0:T(1,128)S(1)}, f32[1,1026]{1,0:T(1,128)S(1)}, u32[]{:S(2)}, u32[]{:S(2)}) collective-permute-start(f32[1,1026]{1,0:T(1,128)S(1)} %get-tuple-element.65), channel_id=1, source_target_pairs={{0,1},{1,2},{2,3},{3,4},{4,5},{5,6},{6,7},{8,9},{9,10},{10,11},{11... | collective-permute-start | bytes 12320 | tf_op jit(solution)/shard_map/ppermute | solution.py:20
  92.0 3.8 %fusion.27 = (f32[256,1024]{1,0:T(8,128)S(1)}, f32[256,1024]{1,0:T(8,128)S(1)}) fusion(f32[256,1024]{1,0:T(8,128)} %get-tuple-element.56, f32[256,1024]{1,0:T(8,128)S(1)} %fusion.32, f32[256,1]{1,0:T(8,128)S(1)} %collective-permute-done.11, f32[256,1]{1,0:T(8,128)S(1)} %collective-permute-done.10, s32[256,1024]{1,0:T(8,128)S(1)} %copy-done, ...), kind=kLoop, calls=%fused_computation.42 | loop fusion | flops 3932160 | bytes 8400912 | tf_op jit(solution)/shard_map/mul | solution.py:59
  97.9 5.5 %collective-permute-start.17 = (f32[256,1]{1,0:T(8,128)S(1)}, f32[256,1]{1,0:T(8,128)}, u32[]{:S(2)}, u32[]{:S(2)}) collective-permute-start(f32[256,1]{1,0:T(8,128)S(1)} %get-tuple-element.78), channel_id=1, source_target_pairs={{8,0},{16,8},{24,16},{32,24},{40,32},{48,40},{56,48},{64,56},{72,6... | collective-permute-start | bytes 3080 | tf_op jit(solution)/shard_map/ppermute | solution.py:21
  114.4 5.3 %collective-permute-start.19 = (f32[1,1026]{1,0:T(1,128)S(1)}, f32[1,1026]{1,0:T(1,128)S(1)}, u32[]{:S(2)}, u32[]{:S(2)}) collective-permute-start(f32[1,1026]{1,0:T(1,128)S(1)} %get-tuple-element.63), channel_id=1, source_target_pairs={{0,1},{1,2},{2,3},{3,4},{4,5},{5,6},{6,7},{8,9},{9,10},{10,11},{11... | collective-permute-start | bytes 12320 | tf_op jit(solution)/shard_map/ppermute | solution.py:20
  120.4 3.6 %fusion.18 = f32[256,1024]{1,0:T(8,128)S(1)} fusion(f32[256,1024]{1,0:T(8,128)S(1)} %fusion.32, f32[256,1026]{1,0:T(8,128)} %concatenate.127, f32[1,1026]{1,0:T(1,128)S(1)} %collective-permute-done.19, f32[1,1026]{1,0:T(1,128)S(1)} %collective-permute-done.18, f32[256,1024]{1,0:T(8,128)} %copy-done.5, f32[256,1]{1,0:T(8,128)S(1)} %collective-permute-done.13, ...), kind=kLoop, calls=%fused_computation.27 | loop fusion | flops 2883584 | bytes 5255184 | tf_op jit(solution)/shard_map/mul | solution.py:69
  124.1 3.8 %collective-permute-start.20 = (f32[256,1]{1,0:T(8,128)S(1)}, f32[256,1]{1,0:T(8,128)S(1)}, u32[]{:S(2)}, u32[]{:S(2)}) collective-permute-start(f32[256,1]{1,0:T(8,128)S(1)} %get-tuple-element.74), channel_id=1, source_target_pairs={{8,0},{16,8},{24,16},{32,24},{40,32},{48,40},{56,48},{64,56},{72,6... | collective-permute-start | bytes 3080 | tf_op jit(solution)/shard_map/ppermute | solution.py:21
  129.8 5.9 %collective-permute-done.21 = f32[256,1]{1,0:T(8,128)S(1)} collective-permute-done((f32[256,1]{1,0:T(8,128)S(1)}, f32[256,1]{1,0:T(8,128)S(1)}, u32[]{:S(2)}, u32[]{:S(2)}) %collective-permute-start.21) | collective-permute-done | bytes 1056 | tf_op jit(solution)/shard_map/ppermute | solution.py:20
  139.8 5.6 %collective-permute-start.25 = (f32[1,1026]{1,0:T(1,128)S(1)}, f32[1,1026]{1,0:T(1,128)S(1)}, u32[]{:S(2)}, u32[]{:S(2)}) collective-permute-start(f32[1,1026]{1,0:T(1,128)S(1)} %get-tuple-element.61), channel_id=1, source_target_pairs={{0,1},{1,2},{2,3},{3,4},{4,5},{5,6},{6,7},{8,9},{9,10},{10,11},{11... | collective-permute-start | bytes 12320 | tf_op jit(solution)/shard_map/ppermute | solution.py:20
  146.1 3.5 %fusion.13 = (f32[256,1024]{1,0:T(8,128)S(1)}, f32[256,1024]{1,0:T(8,128)S(1)}) fusion(f32[256,1024]{1,0:T(8,128)} %copy-done.5, f32[256,1024]{1,0:T(8,128)S(1)} %fusion.18, f32[256,1]{1,0:T(8,128)S(1)} %collective-permute-done.21, f32[256,1]{1,0:T(8,128)S(1)} %collective-permute-done.20, s32[256,1024]{1,0:T(8,128)S(1)} %copy-done, f32[256,1024]{1,0:T(8,128)} %param.17, ...), kind=kLoop, calls=%fused_computation.20 | loop fusion | flops 3932160 | bytes 8400912 | tf_op jit(solution)/shard_map/mul | solution.py:59
  152.7 5.5 %collective-permute-start.27 = (f32[256,1]{1,0:T(8,128)S(1)}, f32[256,1]{1,0:T(8,128)}, u32[]{:S(2)}, u32[]{:S(2)}) collective-permute-start(f32[256,1]{1,0:T(8,128)S(1)} %get-tuple-element.72), channel_id=1, source_target_pairs={{8,0},{16,8},{24,16},{32,24},{40,32},{48,40},{56,48},{64,56},{72,6... | collective-permute-start | bytes 3080 | tf_op jit(solution)/shard_map/ppermute | solution.py:21
  160.8 3.5 %collective-permute-start.23 = (f32[256,1]{1,0:T(8,128)}, f32[256,1]{1,0:T(8,128)S(1)}, u32[]{:S(2)}, u32[]{:S(2)}) collective-permute-start(f32[256,1]{1,0:T(8,128)} %get-tuple-element.71), channel_id=1, source_target_pairs={{0,8},{8,16},{16,24},{24,32},{32,40},{40,48},{48,56},{56,64},{64,7... | collective-permute-start | bytes 3080 | tf_op jit(solution)/shard_map/ppermute | solution.py:20
  169.4 5.5 %collective-permute-start.29 = (f32[1,1026]{1,0:T(1,128)S(1)}, f32[1,1026]{1,0:T(1,128)S(1)}, u32[]{:S(2)}, u32[]{:S(2)}) collective-permute-start(f32[1,1026]{1,0:T(1,128)S(1)} %get-tuple-element.59), channel_id=1, source_target_pairs={{0,1},{1,2},{2,3},{3,4},{4,5},{5,6},{6,7},{8,9},{9,10},{10,11},{11... | collective-permute-start | bytes 12320 | tf_op jit(solution)/shard_map/ppermute | solution.py:20
  181.8 5.5 %collective-permute-start.31 = (f32[20,2]{1,0:T(8,128)S(1)}, f32[20,2]{1,0:T(8,128)S(1)}, u32[]{:S(2)}, u32[]{:S(2)}) collective-permute-start(f32[20,2]{1,0:T(8,128)S(1)} %get-tuple-element.91), channel_id=1, source_target_pairs={{8,0},{16,8},{24,16},{32,24},{40,32},{48,40},{56,48},{64,56},{72,6... | collective-permute-start | bytes 488 | tf_op jit(solution)/shard_map/ppermute | solution.py:21
  188.2 5.3 %collective-permute-start.32 = (f32[2,72]{1,0:T(2,128)S(1)}, f32[2,72]{1,0:T(2,128)S(1)}, u32[]{:S(2)}, u32[]{:S(2)}) collective-permute-start(f32[2,72]{1,0:T(2,128)S(1)} %get-tuple-element.89), channel_id=1, source_target_pairs={{0,1},{1,2},{2,3},{3,4},{4,5},{5,6},{6,7},{8,9},{9,10},{10,11},{11... | collective-permute-start | bytes 1736 | tf_op jit(solution)/shard_map/ppermute | solution.py:20
  (112 shorter events, 82.1 us)
Async XLA Ops:
  1.7 9.8 %collective-permute-start = (f32[256,1]{1,0:T(8,128)S(1)}, f32[256,1]{1,0:T(8,128)S(1)}, u32[]{:S(2)}, u32[]{:S(2)}) collective-permute-start(f32[256,1]{1,0:T(8,128)S(1)} %get-tuple-element.86), channel_id=1, source_target_pairs={{8,0},{16,8},{24,16},{32,24},{40,32},{48,40},{56,48},{64,56},{72,6... | collective-permute-start | bytes 3080 | tf_op jit(solution)/shard_map/ppermute | solution.py:21
  9.4 8.0 %collective-permute-start.1 = (f32[256,1]{1,0:T(8,128)S(1)}, f32[256,1]{1,0:T(8,128)S(1)}, u32[]{:S(2)}, u32[]{:S(2)}) collective-permute-start(f32[256,1]{1,0:T(8,128)S(1)} %get-tuple-element.87), channel_id=1, source_target_pairs={{0,8},{8,16},{16,24},{24,32},{32,40},{40,48},{48,56},{56,64},{64,7... | collective-permute-start | bytes 3080 | tf_op jit(solution)/shard_map/ppermute | solution.py:20
  20.5 7.0 %collective-permute-start.4 = (f32[1,1026]{1,0:T(1,128)S(1)}, f32[1,1026]{1,0:T(1,128)S(1)}, u32[]{:S(2)}, u32[]{:S(2)}) collective-permute-start(f32[1,1026]{1,0:T(1,128)S(1)} %get-tuple-element.68), channel_id=1, source_target_pairs={{1,0},{2,1},{3,2},{4,3},{5,4},{6,5},{7,6},{9,8},{10,9},{11,10},{12... | collective-permute-start | bytes 12320 | tf_op jit(solution)/shard_map/ppermute | solution.py:21
  33.2 9.4 %collective-permute-start.6 = (f32[256,1]{1,0:T(8,128)S(1)}, f32[256,1]{1,0:T(8,128)S(1)}, u32[]{:S(2)}, u32[]{:S(2)}) collective-permute-start(f32[256,1]{1,0:T(8,128)S(1)} %get-tuple-element.85), channel_id=1, source_target_pairs={{0,8},{8,16},{16,24},{24,32},{32,40},{40,48},{48,56},{56,64},{64,7... | collective-permute-start | bytes 3080 | tf_op jit(solution)/shard_map/ppermute | solution.py:20
  35.1 8.6 %collective-permute-start.7 = (f32[256,1]{1,0:T(8,128)S(1)}, f32[256,1]{1,0:T(8,128)S(1)}, u32[]{:S(2)}, u32[]{:S(2)}) collective-permute-start(f32[256,1]{1,0:T(8,128)S(1)} %get-tuple-element.84), channel_id=1, source_target_pairs={{8,0},{16,8},{24,16},{32,24},{40,32},{48,40},{56,48},{64,56},{72,6... | collective-permute-start | bytes 3080 | tf_op jit(solution)/shard_map/ppermute | solution.py:21
  45.9 22.2 %collective-permute-start.8 = (f32[1,1026]{1,0:T(1,128)S(1)}, f32[1,1026]{1,0:T(1,128)S(1)}, u32[]{:S(2)}, u32[]{:S(2)}) collective-permute-start(f32[1,1026]{1,0:T(1,128)S(1)} %get-tuple-element.66), channel_id=1, source_target_pairs={{1,0},{2,1},{3,2},{4,3},{5,4},{6,5},{7,6},{9,8},{10,9},{11,10},{12... | collective-permute-start | bytes 12320 | tf_op jit(solution)/shard_map/ppermute | solution.py:21
  48.4 19.7 %collective-permute-start.9 = (f32[1,1026]{1,0:T(1,128)S(1)}, f32[1,1026]{1,0:T(1,128)S(1)}, u32[]{:S(2)}, u32[]{:S(2)}) collective-permute-start(f32[1,1026]{1,0:T(1,128)S(1)} %get-tuple-element.67), channel_id=1, source_target_pairs={{0,1},{1,2},{2,3},{3,4},{4,5},{5,6},{6,7},{8,9},{9,10},{10,11},{11... | collective-permute-start | bytes 12320 | tf_op jit(solution)/shard_map/ppermute | solution.py:20
  53.0 8.8 %collective-permute-start.2 = (f32[256,1]{1,0:T(8,128)S(1)}, f32[256,1]{1,0:T(8,128)S(1)}, u32[]{:S(2)}, u32[]{:S(2)}) collective-permute-start(f32[256,1]{1,0:T(8,128)S(1)} %get-tuple-element.82), channel_id=1, source_target_pairs={{8,0},{16,8},{24,16},{32,24},{40,32},{48,40},{56,48},{64,56},{72,6... | collective-permute-start | bytes 3080 | tf_op jit(solution)/shard_map/ppermute | solution.py:21
  59.2 8.8 %collective-permute-start.3 = (f32[256,1]{1,0:T(8,128)S(1)}, f32[256,1]{1,0:T(8,128)S(1)}, u32[]{:S(2)}, u32[]{:S(2)}) collective-permute-start(f32[256,1]{1,0:T(8,128)S(1)} %get-tuple-element.83), channel_id=1, source_target_pairs={{0,8},{8,16},{16,24},{24,32},{32,40},{40,48},{48,56},{56,64},{64,7... | collective-permute-start | bytes 3080 | tf_op jit(solution)/shard_map/ppermute | solution.py:20
  73.7 8.7 %collective-permute-start.11 = (f32[256,1]{1,0:T(8,128)S(1)}, f32[256,1]{1,0:T(8,128)S(1)}, u32[]{:S(2)}, u32[]{:S(2)}) collective-permute-start(f32[256,1]{1,0:T(8,128)S(1)} %get-tuple-element.81), channel_id=1, source_target_pairs={{0,8},{8,16},{16,24},{24,32},{32,40},{40,48},{48,56},{56,64},{64,7... | collective-permute-start | bytes 3080 | tf_op jit(solution)/shard_map/ppermute | solution.py:20
  96.0 13.5 %collective-permute-start.16 = (f32[256,1]{1,0:T(8,128)S(1)}, f32[256,1]{1,0:T(8,128)S(1)}, u32[]{:S(2)}, u32[]{:S(2)}) collective-permute-start(f32[256,1]{1,0:T(8,128)S(1)} %get-tuple-element.79), channel_id=1, source_target_pairs={{0,8},{8,16},{16,24},{24,32},{32,40},{40,48},{48,56},{56,64},{64,7... | collective-permute-start | bytes 3080 | tf_op jit(solution)/shard_map/ppermute | solution.py:20
  97.9 11.5 %collective-permute-start.17 = (f32[256,1]{1,0:T(8,128)S(1)}, f32[256,1]{1,0:T(8,128)}, u32[]{:S(2)}, u32[]{:S(2)}) collective-permute-start(f32[256,1]{1,0:T(8,128)S(1)} %get-tuple-element.78), channel_id=1, source_target_pairs={{8,0},{16,8},{24,16},{32,24},{40,32},{48,40},{56,48},{64,56},{72,6... | collective-permute-start | bytes 3080 | tf_op jit(solution)/shard_map/ppermute | solution.py:21
  104.1 15.5 %collective-permute-start.12 = (f32[256,1]{1,0:T(8,128)}, f32[256,1]{1,0:T(8,128)S(1)}, u32[]{:S(2)}, u32[]{:S(2)}) collective-permute-start(f32[256,1]{1,0:T(8,128)} %get-tuple-element.76), channel_id=1, source_target_pairs={{8,0},{16,8},{24,16},{32,24},{40,32},{48,40},{56,48},{64,56},{72,6... | collective-permute-start | bytes 3080 | tf_op jit(solution)/shard_map/ppermute | solution.py:21
  106.0 13.6 %collective-permute-start.13 = (f32[256,1]{1,0:T(8,128)}, f32[256,1]{1,0:T(8,128)S(1)}, u32[]{:S(2)}, u32[]{:S(2)}) collective-permute-start(f32[256,1]{1,0:T(8,128)} %get-tuple-element.77), channel_id=1, source_target_pairs={{0,8},{8,16},{16,24},{24,32},{32,40},{40,48},{48,56},{56,64},{64,7... | collective-permute-start | bytes 3080 | tf_op jit(solution)/shard_map/ppermute | solution.py:20
  112.4 7.3 %collective-permute-start.18 = (f32[1,1026]{1,0:T(1,128)S(1)}, f32[1,1026]{1,0:T(1,128)S(1)}, u32[]{:S(2)}, u32[]{:S(2)}) collective-permute-start(f32[1,1026]{1,0:T(1,128)S(1)} %get-tuple-element.62), channel_id=1, source_target_pairs={{1,0},{2,1},{3,2},{4,3},{5,4},{6,5},{7,6},{9,8},{10,9},{11,10},{12... | collective-permute-start | bytes 12320 | tf_op jit(solution)/shard_map/ppermute | solution.py:21
  127.8 7.8 %collective-permute-start.21 = (f32[256,1]{1,0:T(8,128)S(1)}, f32[256,1]{1,0:T(8,128)S(1)}, u32[]{:S(2)}, u32[]{:S(2)}) collective-permute-start(f32[256,1]{1,0:T(8,128)S(1)} %get-tuple-element.75), channel_id=1, source_target_pairs={{0,8},{8,16},{16,24},{24,32},{32,40},{40,48},{48,56},{56,64},{64,7... | collective-permute-start | bytes 3080 | tf_op jit(solution)/shard_map/ppermute | solution.py:20
  137.9 7.6 %collective-permute-start.24 = (f32[1,1026]{1,0:T(1,128)S(1)}, f32[1,1026]{1,0:T(1,128)S(1)}, u32[]{:S(2)}, u32[]{:S(2)}) collective-permute-start(f32[1,1026]{1,0:T(1,128)S(1)} %get-tuple-element.60), channel_id=1, source_target_pairs={{1,0},{2,1},{3,2},{4,3},{5,4},{6,5},{7,6},{9,8},{10,9},{11,10},{12... | collective-permute-start | bytes 12320 | tf_op jit(solution)/shard_map/ppermute | solution.py:21
  150.7 13.6 %collective-permute-start.26 = (f32[256,1]{1,0:T(8,128)S(1)}, f32[256,1]{1,0:T(8,128)S(1)}, u32[]{:S(2)}, u32[]{:S(2)}) collective-permute-start(f32[256,1]{1,0:T(8,128)S(1)} %get-tuple-element.73), channel_id=1, source_target_pairs={{0,8},{8,16},{16,24},{24,32},{32,40},{40,48},{48,56},{56,64},{64,7... | collective-permute-start | bytes 3080 | tf_op jit(solution)/shard_map/ppermute | solution.py:20
  152.7 11.7 %collective-permute-start.27 = (f32[256,1]{1,0:T(8,128)S(1)}, f32[256,1]{1,0:T(8,128)}, u32[]{:S(2)}, u32[]{:S(2)}) collective-permute-start(f32[256,1]{1,0:T(8,128)S(1)} %get-tuple-element.72), channel_id=1, source_target_pairs={{8,0},{16,8},{24,16},{32,24},{40,32},{48,40},{56,48},{64,56},{72,6... | collective-permute-start | bytes 3080 | tf_op jit(solution)/shard_map/ppermute | solution.py:21
  158.9 16.0 %collective-permute-start.22 = (f32[256,1]{1,0:T(8,128)}, f32[256,1]{1,0:T(8,128)S(1)}, u32[]{:S(2)}, u32[]{:S(2)}) collective-permute-start(f32[256,1]{1,0:T(8,128)} %get-tuple-element.70), channel_id=1, source_target_pairs={{8,0},{16,8},{24,16},{32,24},{40,32},{48,40},{56,48},{64,56},{72,6... | collective-permute-start | bytes 3080 | tf_op jit(solution)/shard_map/ppermute | solution.py:21
  160.8 14.1 %collective-permute-start.23 = (f32[256,1]{1,0:T(8,128)}, f32[256,1]{1,0:T(8,128)S(1)}, u32[]{:S(2)}, u32[]{:S(2)}) collective-permute-start(f32[256,1]{1,0:T(8,128)} %get-tuple-element.71), channel_id=1, source_target_pairs={{0,8},{8,16},{16,24},{24,32},{32,40},{40,48},{48,56},{56,64},{64,7... | collective-permute-start | bytes 3080 | tf_op jit(solution)/shard_map/ppermute | solution.py:20
  167.5 7.5 %collective-permute-start.28 = (f32[1,1026]{1,0:T(1,128)S(1)}, f32[1,1026]{1,0:T(1,128)S(1)}, u32[]{:S(2)}, u32[]{:S(2)}) collective-permute-start(f32[1,1026]{1,0:T(1,128)S(1)} %get-tuple-element.58), channel_id=1, source_target_pairs={{1,0},{2,1},{3,2},{4,3},{5,4},{6,5},{7,6},{9,8},{10,9},{11,10},{12... | collective-permute-start | bytes 12320 | tf_op jit(solution)/shard_map/ppermute | solution.py:21
  179.9 8.0 %collective-permute-start.30 = (f32[20,2]{1,0:T(8,128)S(1)}, f32[20,2]{1,0:T(8,128)S(1)}, u32[]{:S(2)}, u32[]{:S(2)}) collective-permute-start(f32[20,2]{1,0:T(8,128)S(1)} %get-tuple-element.90), channel_id=1, source_target_pairs={{0,8},{8,16},{16,24},{24,32},{32,40},{40,48},{48,56},{56,64},{64,7... | collective-permute-start | bytes 488 | tf_op jit(solution)/shard_map/ppermute | solution.py:20
  188.2 7.3 %collective-permute-start.32 = (f32[2,72]{1,0:T(2,128)S(1)}, f32[2,72]{1,0:T(2,128)S(1)}, u32[]{:S(2)}, u32[]{:S(2)}) collective-permute-start(f32[2,72]{1,0:T(2,128)S(1)} %get-tuple-element.89), channel_id=1, source_target_pairs={{0,1},{1,2},{2,3},{3,4},{4,5},{5,6},{6,7},{8,9},{9,10},{10,11},{11... | collective-permute-start | bytes 1736 | tf_op jit(solution)/shard_map/ppermute | solution.py:20
  (21 other events, 192.3 us)
where the time goes:
time: 202 us; the launch traced here: 200 us
  starting transfers between devices  118 us (58%)
  waiting for transfers between devices  33.5 us (17%)
  other arithmetic  24.6 us (12%)
  local copies, waits for them, and re-layouts  21.5 us (11%)
    ppermute x17, starting transfers between devices, with_halo(): after = lax.ppermute(initial, axis, down)  62.5 us
    ppermute x17, starting transfers between devices, with_halo(): before = lax.ppermute(last, axis, up)  55.6 us
    ppermute x17, waiting for transfers between devices, with_halo(): before = lax.ppermute(last, axis, up)  27.3 us
    mul x3, other arithmetic, local(): wet_fraction * (eastward + courant * wet_depth * (padded[1:-1, 2:] - padd...  12.1 us
    concatenate x6, local copies, waits for them, and re-layouts, with_halo(): array = jnp.concatenate([before, array, after], axis=dim)  11.1 us
    mul x3, other arithmetic, local(): wet_fraction * (surface_height + courant * (east_pad[1:-1, 2:] - east_pad...  10.1 us
    slice x15, local copies, waits for them, and re-layouts, with_halo(): initial = lax.slice_in_dim(array, 0, width, axis=dim)  8.86 us
    ppermute x17, waiting for transfers between devices, with_halo(): after = lax.ppermute(initial, axis, down)  6.23 us
  transfers between devices with their start and end apart: 34, of which 16 were waited for; matrix products, arithmetic and copies ran while one was open for 5% of the time, Pallas kernels for 0%

commit v1 on v0

v1 whole, which is shorter than its diff:
```python
import jax
import jax.numpy as jnp
from jax import lax
from jax.experimental import pallas as pl
from jax.experimental.pallas import tpu as pltpu
from jax.sharding import PartitionSpec as P

SPACING = 16
LANES = 128
HALO = 8
BLOCK = 16
F32 = jnp.float32

SOUTH, NORTH, WEST, EAST = (-1, 0), (1, 0), (0, -1), (0, 1)
SW, SE, NW, NE = (-1, -1), (-1, 1), (1, -1), (1, 1)
NEIGHBOURS = (SOUTH, NORTH, WEST, EAST, SW, SE, NW, NE)


def spline_weight(arg):
    mag = jnp.abs(arg)
    inner = 2.0 / 3.0 - mag * mag + 0.5 * mag * mag * mag
    outer = (2.0 - mag) * (2.0 - mag) * (2.0 - mag) / 6.0
    return jnp.where(mag < 1.0, inner, jnp.where(mag < 2.0, outer, 0.0 * mag))


def lanes_of(shape):
    return lax.broadcasted_iota(jnp.int32, shape, 1)


def left(x, k):
    return pltpu.roll(x, x.shape[1] - k, axis=1)


def right(x, k):
    return pltpu.roll(x, k, axis=1)


def below(x, following, k):
    return jnp.concatenate([x, following], axis=0)[k : k + x.shape[0]]


def above(preceding, x, k):
    return jnp.concatenate([preceding, x], axis=0)[HALO - k : HALO - k + x.shape[0]]


def kernel(
    s_in, e_in, n_in, d_in, w_in, active,
    s_out, e_out, n_out, grad,
    S, E, N, CX, CY, M, W, R, PART,
    pack_w, pack_e, got_w, got_e, corner, fold,
    load_sem, send_sem, recv_sem,
):
    rows, cols = s_out.shape
    tall = rows + 2 * HALO
    tiles = cols // LANES
    quarter = rows // 4
    nlat, nlon = lax.axis_size("lat"), lax.axis_size("lon")
    lat, lon = lax.axis_index("lat"), lax.axis_index("lon")

    def has(offset):
        a, b = lat + offset[0], lon + offset[1]
        return (a >= 0) & (a < nlat) & (b >= 0) & (b < nlon)

    def opposite(offset):
        return (-offset[0], -offset[1])

    regions = (
        (0, rows, 0, LANES),
        (0, rows, cols - LANES, LANES),
        (0, HALO, LANES, cols - 2 * LANES),
        (rows - HALO, HALO, LANES, cols - 2 * LANES),
        (HALO, rows - 2 * HALO, LANES, cols - 2 * LANES),
    )
    loads = []
    for k, (r, h, c, w) in enumerate(regions):
        group = []
        for a, (src, dst) in enumerate(((w_in, W), (d_in, CX), (e_in, E), (n_in, N), (s_in, S))):
            base = 0 if dst is W else HALO
            group.append(
                pltpu.make_async_copy(
                    src.at[pl.ds(r, h), pl.ds(c, w)],
                    dst.at[pl.ds(base + r, h), pl.ds(c, w)],
                    load_sem.at[k * 5 + a],
                )
            )
        loads.append(group)
    for group in loads:
        for copy in group:
            copy.start()

    barrier = pltpu.get_barrier_semaphore()
    count = jnp.int32(0)
    for offset in NEIGHBOURS:
        count = count + has(offset).astype(jnp.int32)

        @pl.when(has(offset))
        def _(offset=offset):
            pl.semaphore_signal(
                barrier, inc=1,
                device_id={"lat": lat + offset[0], "lon": lon + offset[1]},
                device_id_type=pl.DeviceIdType.MESH,
            )

    def messages(items, first):
        made = []
        for k, (src, dst, offset) in enumerate(items):
            made.append((
                pltpu.make_async_remote_copy(
                    src_ref=src, dst_ref=dst,
                    send_sem=send_sem.at[first + k], recv_sem=recv_sem.at[first + k],
                    device_id={"lat": lat + offset[0], "lon": lon + offset[1]},
                    device_id_type=pl.DeviceIdType.MESH,
                ),
                offset,
            ))
        return made

    def start(made):
        for copy, offset in made:
            @pl.when(has(offset))
            def _(copy=copy):
                copy.start()

    def finish(made):
        for copy, offset in made:
            @pl.when(has(opposite(offset)))
            def _(copy=copy):
                copy.wait_recv()

            @pl.when(has(offset))
            def _(copy=copy):
                copy.wait_send()

    fields = (S, E, N, CX)
    body = pl.ds(0, cols)
    low, high = pl.ds(0, HALO), pl.ds(HALO + rows, HALO)
    first_rows, last_rows = pl.ds(HALO, HALO), pl.ds(rows, HALO)
    side = [(pack_w, got_e, WEST), (pack_e, got_w, EAST)]
    side += [
        (pack_w.at[pl.ds(0, HALO)], corner.at[3], SW),
        (pack_e.at[pl.ds(0, HALO)], corner.at[2], SE),
        (pack_w.at[pl.ds(quarter - HALO, HALO)], corner.at[1], NW),
        (pack_e.at[pl.ds(quarter - HALO, HALO)], corner.at[0], NE),
    ]
    rim = [(f.at[first_rows, body], f.at[high, body], SOUTH) for f in fields]
    rim += [(f.at[last_rows, body], f.at[low, body], NORTH) for f in fields]
    rim = messages(rim, 0)
    side = messages(side, len(rim))

    @pl.when(lat == 0)
    def _():
        for f in fields:
            f[0:HALO, 0:cols] = jnp.zeros((HALO, cols), F32)
        fold[0] = jnp.zeros_like(fold[0])

    @pl.when(lat == nlat - 1)
    def _():
        for f in fields:
            f[HALO + rows : tall, 0:cols] = jnp.zeros((HALO, cols), F32)
        fold[1] = jnp.zeros_like(fold[1])

    for pack, offset, k in ((got_w, WEST, 2), (got_e, EAST, 3)):
        @pl.when(jnp.logical_not(has(offset)))
        def _(pack=pack, k=k):
            pack[...] = jnp.zeros_like(pack)
            fold[k] = jnp.zeros_like(fold[k])

    for k, offset in enumerate((SW, SE, NW, NE)):
        @pl.when(jnp.logical_not(has(offset)))
        def _(k=k):
            corner[k] = jnp.zeros_like(corner[k])
            fold[4 + k] = jnp.zeros_like(fold[4 + k])

    for f in (S, N, CX):
        f[tall : tall + HALO, :] = jnp.zeros((HALO, cols + LANES), F32)
    R[...] = jnp.zeros_like(R)

    def prepare(r, h, c, w):
        here = (pl.ds(HALO + r, h), pl.ds(c, w))
        wet = W[pl.ds(r, h), pl.ds(c, w)].astype(F32)
        half = 0.5 * wet
        M[here] = half
        CX[here] = CX[here] * half
        E[here] = E[here] * wet
        N[here] = N[here] * wet

    for k in (0, 1, 2, 3):
        for copy in loads[k]:
            copy.wait()
        prepare(*regions[k])

    lane = lanes_of((quarter, LANES))
    for pack, tile, turn in ((pack_w, 0, 0), (pack_e, tiles - 1, 1)):
        total = jnp.zeros((quarter, LANES), F32)
        for a, f in enumerate(fields):
            for b in range(4):
                g = 4 * b + a
                piece = f[HALO + b * quarter : HALO + (b + 1) * quarter, tile * LANES : (tile + 1) * LANES]
                shift = 8 * (g + turn) % LANES
                piece = piece if shift == 0 else right(piece, shift)
                total = jnp.where((lane >= 8 * g) & (lane < 8 * g + 8), piece, total)
        pack[...] = total

    pl.semaphore_wait(barrier, count)
    start(side)
    start(rim)

    for copy in loads[4]:
        copy.wait()

    inner = regions[4]

    def prepare_block(j, carry):
        prepare(pl.multiple_of(HALO + j * BLOCK, HALO), BLOCK, inner[2], inner[3])
        return carry

    lax.fori_loop(0, inner[1] // BLOCK, prepare_block, 0)

    shape = (LANES, LANES)
    at = (lax.broadcasted_iota(jnp.int32, shape, 0).astype(F32) + 0.5) / SPACING
    column_weight = spline_weight(at - (lanes_of(shape).astype(F32) - 2.0 + 0.5))
    within = (lax.broadcasted_iota(jnp.int32, (BLOCK, LANES), 0).astype(F32) + 0.5) / SPACING
    row_weight = [jnp.tile(spline_weight(within + 1.0 - m), (1, tiles)) for m in range(4)]

    finish(side)
    finish(rim)

    ring = pl.ds(cols, LANES)

    def unpack(east, west, g):
        x = lanes_of(east.shape)
        e = east if g == 0 else right(east, LANES - 8 * g)
        w = right(west, (LANES - 8 * (g + 1)) % LANES)
        return jnp.where(x < 8, e, jnp.where(x >= LANES - 8, w, 0.0))

    for a, f in enumerate(fields):
        for b in range(4):
            f[HALO + b * quarter : HALO + (b + 1) * quarter, ring] = unpack(got_e[...], got_w[...], 4 * b + a)
        f[0:HALO, ring] = unpack(corner[1], corner[0], 12 + a)
        f[HALO + rows : tall, ring] = unpack(corner[3], corner[2], a)
    M[:, ring] = jnp.where(CX[0:tall, ring] > 0.0, 0.5, 0.0)
    for span in (low, high):
        M[span, body] = jnp.where(CX[span, body] > 0.0, 0.5, 0.0)

    blocks = tall // BLOCK
    wide = cols + LANES

    def advance(s, s_next, e, n, cx, cy, m, n_before, first):
        e = e + cx * (left(s, 2) - s)
        n = n + cy * (below(s, s_next, 2) - s)
        change = (e - right(e, 2)) + (n - above(n_before, n, 2))
        s = m * (s + s + change) if first else s + m * change
        return s, e, n

    def first_step(j, n_before):
        r = pl.multiple_of(j * BLOCK, BLOCK)
        here, nxt = pl.ds(r, BLOCK), pl.ds(r + BLOCK, HALO)
        depth = CX[here]
        cx = left(depth, 1)
        cy = below(depth, CX[nxt], 1)
        e = left(E[here], 1)
        n = below(N[here], N[nxt], 1)
        s, e, n = advance(S[here], S[nxt], e, n, cx, cy, M[here], n_before, True)
        S[here], E[here], N[here], CX[here], CY[here] = s, e, n, cx, cy
        return n[BLOCK - HALO :]

    def second_step(j, n_before):
        r = pl.multiple_of(j * BLOCK, BLOCK)
        here, nxt = pl.ds(r, BLOCK), pl.ds(r + BLOCK, HALO)
        s, e, n = advance(S[here], S[nxt], E[here], N[here], CX[here], CY[here], M[here], n_before, False)
        S[here], E[here], N[here] = s, e, n
        return n[BLOCK - HALO :]

    def last_step(j, carry, part=(0, BLOCK)):
        n_before, one, two, three = carry
        r = j * BLOCK if isinstance(j, int) else pl.multiple_of(j * BLOCK, BLOCK)
        here, nxt = pl.ds(r, BLOCK), pl.ds(r + BLOCK, HALO)
        s, e, n = advance(S[here], S[nxt], E[here], N[here], CX[here], CY[here], M[here], n_before, False)
        begin, end = part
        own = r - HALO + begin
        own = own if isinstance(j, int) else pl.multiple_of(own, HALO)
        dst = pl.ds(own, end - begin)
        s = s[begin:end, :cols]
        s_out[dst] = s
        e_out[dst] = right(e, 1)[begin:end, :cols]
        n_out[dst] = above(n_before, n, 1)[begin:end, :cols]
        sums = []
        for weight in row_weight:
            term = s * weight[begin:end]
            sums.append(term if end - begin == HALO else term[:HALO] + term[HALO:])
        R[pl.ds(j, 1), :] = jnp.sum(one + sums[0], axis=0, keepdims=True)
        return n[BLOCK - HALO :], two + sums[1], three + sums[2], sums[3]

    zero = jnp.zeros((HALO, wide), F32)
    lax.fori_loop(0, blocks, first_step, zero)
    lax.fori_loop(0, blocks, second_step, zero)
    none = jnp.zeros((HALO, cols), F32)
    carry = last_step(0, (zero, none, none, none), (HALO, BLOCK))
    carry = lax.fori_loop(1, blocks - 1, last_step, carry)
    carry = last_step(blocks - 1, carry, (0, HALO))
    for k in range(3):
        R[blocks + k : blocks + k + 1, :] = jnp.sum(carry[1 + k], axis=0, keepdims=True)

    points = R.shape[0]
    stacked = jnp.concatenate([R[:, t * LANES : (t + 1) * LANES] for t in range(tiles)], axis=0)
    spread = jnp.dot(stacked, column_weight, precision=lax.Precision.HIGHEST, preferred_element_type=F32)
    own = spread[0:points]
    for t in range(1, tiles):
        own = own + right(spread[t * points : (t + 1) * points], 8 * t)
    PART[...] = own

    top, bottom = pl.ds(0, HALO), pl.ds(points - HALO, HALO)
    cross = [
        (PART.at[bottom], fold.at[0, top], NORTH),
        (PART.at[top], fold.at[1, top], SOUTH),
        (PART, fold.at[2], EAST),
        (PART, fold.at[3], WEST),
        (PART.at[bottom], fold.at[4, top], NE),
        (PART.at[bottom], fold.at[5, top], NW),
        (PART.at[top], fold.at[6, top], SE),
        (PART.at[top], fold.at[7, top], SW),
    ]
    cross = messages(cross, len(rim) + len(side))
    start(cross)
    finish(cross)

    row = lax.broadcasted_iota(jnp.int32, (HALO, LANES), 0)
    lane = lanes_of((points, LANES))

    def with_rows(middle, south, north):
        south = jnp.where((row == 2) | (row == 3), south, 0.0)
        north = jnp.where(row < 2, north, 0.0)
        return jnp.concatenate(
            [middle[:HALO] + south, middle[HALO : points - HALO], middle[points - HALO :] + north], axis=0
        )

    mine = with_rows(own, fold[0, 0:HALO], fold[1, 0:HALO])
    west = with_rows(fold[2], fold[4, 0:HALO], fold[6, 0:HALO])
    east = with_rows(fold[3], fold[5, 0:HALO], fold[7, 0:HALO])
    half = cols // SPACING
    west = left(west, half)
    east = right(east, half)
    mine = mine + jnp.where((lane == 2) | (lane == 3), west, 0.0)
    mine = mine + jnp.where((lane == half) | (lane == half + 1), east, 0.0)
    inside = mine[2 : 2 + rows // SPACING, 2 : 2 + half]
    grad[...] = inside * active[...].astype(F32) / SPACING


def local(surface_adjoint, east_adjoint, north_adjoint, water_depth, wet_mask, control_active):
    rows, cols = surface_adjoint.shape
    points = rows // SPACING + 4
    points = (points + 7) // 8 * 8
    tall, wide = rows + 2 * HALO, cols + LANES
    field = pltpu.VMEM((tall + HALO, wide), F32)
    quarter = rows // 4
    whole = pl.BlockSpec(memory_space=pltpu.VMEM)
    in_hbm = pl.BlockSpec(memory_space=pltpu.HBM)
    shape = jax.ShapeDtypeStruct((rows, cols), F32)
    return pl.pallas_call(
        kernel,
        out_shape=(shape, shape, shape, jax.ShapeDtypeStruct(control_active.shape, F32)),
        in_specs=[in_hbm] * 5 + [whole],
        out_specs=(whole,) * 4,
        scratch_shapes=[
            field, field, field, field,
            pltpu.VMEM((tall, wide), F32),
            pltpu.VMEM((tall, wide), F32),
            pltpu.VMEM((rows, cols), jnp.int32),
            pltpu.VMEM((points, cols), F32),
            pltpu.VMEM((points, LANES), F32),
            pltpu.VMEM((quarter, LANES), F32),
            pltpu.VMEM((quarter, LANES), F32),
            pltpu.VMEM((quarter, LANES), F32),
            pltpu.VMEM((quarter, LANES), F32),
            pltpu.VMEM((4, HALO, LANES), F32),
            pltpu.VMEM((8, points, LANES), F32),
            pltpu.SemaphoreType.DMA((25,)),
            pltpu.SemaphoreType.DMA((22,)),
            pltpu.SemaphoreType.DMA((22,)),
        ],
        compiler_params=pltpu.CompilerParams(
            collective_id=0, has_side_effects=True, vmem_limit_bytes=32 * 1024 * 1024
        ),
    )(surface_adjoint, east_adjoint, north_adjoint, water_depth, wet_mask, control_active)


def solution(mesh):
    spec = P("lat", "lon")
    return jax.shard_map(
        local, mesh=mesh, in_specs=(spec,) * 6, out_specs=(spec,) * 4, check_vma=False
    )
```

time: 202 us -> 38.8 us (0.19)
  starting transfers between devices: 118 us -> 0 us
  waiting for transfers between devices: 33.5 us -> 0 us
  Pallas kernels: 0 us -> 27.5 us
  other arithmetic: 24.6 us -> 0 us
  local copies, waits for them, and re-layouts: 21.5 us -> 10.3 us
    ppermute x34 -> x0, starting transfers between devices: 118 us -> none  [the longest x17 62.5 us: with_halo(): after = lax.ppermute(initial, axis, down)]
    ppermute x34 -> x0, waiting for transfers between devices: 33.5 us -> none  [the longest x17 27.3 us: with_halo(): before = lax.ppermute(last, axis, up)]
    pallas_call x0 -> x1, Pallas kernels: none -> 27.5 us  [local(): pl.pallas_call(kernel, out_shape=(shape, shape, shape, jax.ShapeDtypeStru...]
    mul x6 -> x0, other arithmetic: 22.2 us -> none  [the longest x3 12.1 us: local(): wet_fraction * (eastward + courant * wet_depth * (padded[1:-1, 2:] - padd...]
    concatenate x6 -> x0, local copies, waits for them, and re-layouts: 11.1 us -> none  [with_halo(): array = jnp.concatenate([before, array, after], axis=dim)]
    unnamed x22 -> x16, local copies, waits for them, and re-layouts: 1.01 us -> 10.3 us
    slice x18 -> x0, local copies, waits for them, and re-layouts: 9.01 us -> none  [the longest x15 8.86 us: with_halo(): initial = lax.slice_in_dim(array, 0, width, axis=dim)]
  transfers between devices with their start and end apart: 34 -> 0, of which waited for: 16 -> 0; matrix products, arithmetic and copies ran while one was open for 5% -> 0% of each run, Pallas kernels for 0% -> 0%
where the time goes in v1:
time: 38.8 us; the launch traced here: 38.5 us
  Pallas kernels  27.5 us (71%)
  local copies, waits for them, and re-layouts  10.3 us (27%)
  between operations  0.66 us (2%)
    pallas_call x1, Pallas kernels, local(): pl.pallas_call(kernel, out_shape=(shape, shape, shape, jax.ShapeDtypeStru...  27.5 us
    unnamed x16, local copies, waits for them, and re-layouts  10.3 us

profile of v1, /device:TPU:25, one launch (start us, length us, event | category | flops | bytes accessed | tf_op | source)
XLA Modules:
  0.0 38.5 jit_solution(12244217172105210966)
XLA Ops:
  0.6 0.0 copy-start
  0.6 1.2 %copy-done = f32[256,1024]{1,0:T(8,128)S(1)} copy-done((f32[256,1024]{1,0:T(8,128)S(1)}, f32[256,1024]{1,0:T(8,128)}, u32[]{:S(2)}) %copy-start) | copy-done | bytes 1048600
  1.9 0.0 copy-start.1
  1.9 1.2 %copy-done.1 = f32[256,1024]{1,0:T(8,128)S(1)} copy-done((f32[256,1024]{1,0:T(8,128)S(1)}, f32[256,1024]{1,0:T(8,128)}, u32[]{:S(2)}) %copy-start.1) | copy-done | bytes 1048600
  3.1 0.0 copy-start.2
  3.1 1.2 %copy-done.2 = f32[256,1024]{1,0:T(8,128)S(1)} copy-done((f32[256,1024]{1,0:T(8,128)S(1)}, f32[256,1024]{1,0:T(8,128)}, u32[]{:S(2)}) %copy-start.2) | copy-done | bytes 1048600
  4.3 0.0 copy-start.3
  4.3 1.2 %copy-done.3 = f32[256,1024]{1,0:T(8,128)S(1)} copy-done((f32[256,1024]{1,0:T(8,128)S(1)}, f32[256,1024]{1,0:T(8,128)}, u32[]{:S(2)}) %copy-start.3) | copy-done | bytes 1048600
  5.5 0.0 copy-start.4
  5.5 1.2 %copy-done.4 = s32[256,1024]{1,0:T(8,128)S(1)} copy-done((s32[256,1024]{1,0:T(8,128)S(1)}, s32[256,1024]{1,0:T(8,128)}, u32[]{:S(2)}) %copy-start.4) | copy-done | bytes 1048600
  6.8 0.0 copy-start.5
  6.8 0.7 %copy-done.5 = s32[16,64]{1,0:T(8,128)S(1)} copy-done((s32[16,64]{1,0:T(8,128)S(1)}, s32[16,64]{1,0:T(8,128)}, u32[]{:S(2)}) %copy-start.5) | copy-done | bytes 4120
  7.5 27.5 %shard_map.93 = (f32[256,1024]{1,0:T(8,128)S(1)}, f32[256,1024]{1,0:T(8,128)S(1)}, f32[256,1024]{1,0:T(8,128)S(1)}, f32[16,64]{1,0:T(8,128)S(1)}) custom-call(f32[256,1024]{1,0:T(8,128)S(1)} %copy-done, f32[256,1024]{1,0:T(8,128)S(1)} %copy-done.1, f32[256,1024]{1,0:T(8,128)S(1)} %copy-done.2, f32[256,1024]{1,0:T(8,128)S(1)} %copy-done.3, ...), custom_call_target="tpu_custom_call" | custom-call | tf_op jit(solution)/shard_map/pallas_call | solution.py:359
  35.0 1.0 %copy.14 = f32[256,1024]{1,0:T(8,128)} copy(f32[256,1024]{1,0:T(8,128)S(1)} %get-tuple-element.8) | data formatting | bytes 2097152
  35.9 1.0 %copy.15 = f32[256,1024]{1,0:T(8,128)} copy(f32[256,1024]{1,0:T(8,128)S(1)} %get-tuple-element.9) | data formatting | bytes 2097152
  36.9 1.0 %copy.16 = f32[256,1024]{1,0:T(8,128)} copy(f32[256,1024]{1,0:T(8,128)S(1)} %get-tuple-element.10) | data formatting | bytes 2097152
  37.9 0.6 %copy.17 = f32[16,64]{1,0:T(8,128)} copy(f32[16,64]{1,0:T(8,128)S(1)} %get-tuple-element.11) | data formatting | bytes 8192
Async XLA Ops:
  0.6 1.2 %copy-start = (f32[256,1024]{1,0:T(8,128)S(1)}, f32[256,1024]{1,0:T(8,128)}, u32[]{:S(2)}) copy-start(f32[256,1024]{1,0:T(8,128)} %s_in.1) | copy-start | bytes 3145732
  1.9 1.2 %copy-start.1 = (f32[256,1024]{1,0:T(8,128)S(1)}, f32[256,1024]{1,0:T(8,128)}, u32[]{:S(2)}) copy-start(f32[256,1024]{1,0:T(8,128)} %e_in.1) | copy-start | bytes 3145732
  3.1 1.2 %copy-start.2 = (f32[256,1024]{1,0:T(8,128)S(1)}, f32[256,1024]{1,0:T(8,128)}, u32[]{:S(2)}) copy-start(f32[256,1024]{1,0:T(8,128)} %n_in.1) | copy-start | bytes 3145732
  4.3 1.2 %copy-start.3 = (f32[256,1024]{1,0:T(8,128)S(1)}, f32[256,1024]{1,0:T(8,128)}, u32[]{:S(2)}) copy-start(f32[256,1024]{1,0:T(8,128)} %d_in.1) | copy-start | bytes 3145732
  5.5 1.2 %copy-start.4 = (s32[256,1024]{1,0:T(8,128)S(1)}, s32[256,1024]{1,0:T(8,128)}, u32[]{:S(2)}) copy-start(s32[256,1024]{1,0:T(8,128)} %w_in.1) | copy-start | bytes 3145732
  6.8 0.7 %copy-start.5 = (s32[16,64]{1,0:T(8,128)S(1)}, s32[16,64]{1,0:T(8,128)}, u32[]{:S(2)}) copy-start(s32[16,64]{1,0:T(8,128)} %active.1) | copy-start | bytes 12292

commit v2 on v1

--- a/solution.py
+++ b/solution.py
@@ -44,9 +44,9 @@
 
 
 def kernel(
-    s_in, e_in, n_in, d_in, w_in, active,
+    s_in, e_in, n_in, d_in, w_in, a_in,
     s_out, e_out, n_out, grad,
-    S, E, N, CX, CY, M, W, R, PART,
+    S, E, N, CX, CY, M, W, R, PART, active,
     pack_w, pack_e, got_w, got_e, corner, fold,
     load_sem, send_sem, recv_sem,
 ):
@@ -88,6 +88,9 @@
         for copy in group:
             copy.start()
 
+    points_load = pltpu.make_async_copy(a_in, active, load_sem.at[25])
+    points_load.start()
+
     barrier = pltpu.get_barrier_semaphore()
     count = jnp.int32(0)
     for offset in NEIGHBOURS:
@@ -171,7 +174,7 @@
             corner[k] = jnp.zeros_like(corner[k])
             fold[4 + k] = jnp.zeros_like(fold[4 + k])
 
-    for f in (S, N, CX):
+    for f in (S, N, CX, M):
         f[tall : tall + HALO, :] = jnp.zeros((HALO, cols + LANES), F32)
     R[...] = jnp.zeros_like(R)
 
@@ -181,8 +184,6 @@
         half = 0.5 * wet
         M[here] = half
         CX[here] = CX[here] * half
-        E[here] = E[here] * wet
-        N[here] = N[here] * wet
 
     for k in (0, 1, 2, 3):
         for copy in loads[k]:
@@ -219,9 +220,6 @@
     shape = (LANES, LANES)
     at = (lax.broadcasted_iota(jnp.int32, shape, 0).astype(F32) + 0.5) / SPACING
     column_weight = spline_weight(at - (lanes_of(shape).astype(F32) - 2.0 + 0.5))
-    within = (lax.broadcasted_iota(jnp.int32, (BLOCK, LANES), 0).astype(F32) + 0.5) / SPACING
-    row_weight = [jnp.tile(spline_weight(within + 1.0 - m), (1, tiles)) for m in range(4)]
-
     finish(side)
     finish(rim)
 
@@ -238,68 +236,113 @@
             f[HALO + b * quarter : HALO + (b + 1) * quarter, ring] = unpack(got_e[...], got_w[...], 4 * b + a)
         f[0:HALO, ring] = unpack(corner[1], corner[0], 12 + a)
         f[HALO + rows : tall, ring] = unpack(corner[3], corner[2], a)
-    M[:, ring] = jnp.where(CX[0:tall, ring] > 0.0, 0.5, 0.0)
+    M[0:tall, ring] = jnp.where(CX[0:tall, ring] > 0.0, 0.5, 0.0)
     for span in (low, high):
         M[span, body] = jnp.where(CX[span, body] > 0.0, 0.5, 0.0)
 
-    blocks = tall // BLOCK
-    wide = cols + LANES
-
-    def advance(s, s_next, e, n, cx, cy, m, n_before, first):
-        e = e + cx * (left(s, 2) - s)
-        n = n + cy * (below(s, s_next, 2) - s)
-        change = (e - right(e, 2)) + (n - above(n_before, n, 2))
-        s = m * (s + s + change) if first else s + m * change
-        return s, e, n
-
-    def first_step(j, n_before):
-        r = pl.multiple_of(j * BLOCK, BLOCK)
-        here, nxt = pl.ds(r, BLOCK), pl.ds(r + BLOCK, HALO)
-        depth = CX[here]
-        cx = left(depth, 1)
-        cy = below(depth, CX[nxt], 1)
-        e = left(E[here], 1)
-        n = below(N[here], N[nxt], 1)
-        s, e, n = advance(S[here], S[nxt], e, n, cx, cy, M[here], n_before, True)
-        S[here], E[here], N[here], CX[here], CY[here] = s, e, n, cx, cy
-        return n[BLOCK - HALO :]
-
-    def second_step(j, n_before):
-        r = pl.multiple_of(j * BLOCK, BLOCK)
-        here, nxt = pl.ds(r, BLOCK), pl.ds(r + BLOCK, HALO)
-        s, e, n = advance(S[here], S[nxt], E[here], N[here], CX[here], CY[here], M[here], n_before, False)
-        S[here], E[here], N[here] = s, e, n
-        return n[BLOCK - HALO :]
-
-    def last_step(j, carry, part=(0, BLOCK)):
-        n_before, one, two, three = carry
-        r = j * BLOCK if isinstance(j, int) else pl.multiple_of(j * BLOCK, BLOCK)
-        here, nxt = pl.ds(r, BLOCK), pl.ds(r + BLOCK, HALO)
-        s, e, n = advance(S[here], S[nxt], E[here], N[here], CX[here], CY[here], M[here], n_before, False)
-        begin, end = part
-        own = r - HALO + begin
-        own = own if isinstance(j, int) else pl.multiple_of(own, HALO)
-        dst = pl.ds(own, end - begin)
-        s = s[begin:end, :cols]
-        s_out[dst] = s
-        e_out[dst] = right(e, 1)[begin:end, :cols]
-        n_out[dst] = above(n_before, n, 1)[begin:end, :cols]
-        sums = []
-        for weight in row_weight:
-            term = s * weight[begin:end]
-            sums.append(term if end - begin == HALO else term[:HALO] + term[HALO:])
-        R[pl.ds(j, 1), :] = jnp.sum(one + sums[0], axis=0, keepdims=True)
-        return n[BLOCK - HALO :], two + sums[1], three + sums[2], sums[3]
-
-    zero = jnp.zeros((HALO, wide), F32)
-    lax.fori_loop(0, blocks, first_step, zero)
-    lax.fori_loop(0, blocks, second_step, zero)
-    none = jnp.zeros((HALO, cols), F32)
-    carry = last_step(0, (zero, none, none, none), (HALO, BLOCK))
-    carry = lax.fori_loop(1, blocks - 1, last_step, carry)
-    carry = last_step(blocks - 1, carry, (0, HALO))
-    for k in range(3):
-        R[blocks + k : blocks + k + 1, :] = jnp.sum(carry[1 + k], axis=0, keepdims=True)
+    count_tiles = tiles + 1
+
+    def spread_of(x, k, height):
+        return [pltpu.roll(v, k % LANES, axis=1) for v in x], lanes_of((height, LANES))
+
+    def from_right(x, k):
+        turned, at = spread_of(x, -k, x[0].shape[0])
+        n = len(x)
+        return [jnp.where(at < LANES - k, turned[t], turned[(t + 1) % n]) for t in range(n)]
+
+    def from_left(x, k):
+        turned, at = spread_of(x, k, x[0].shape[0])
+        n = len(x)
+        return [jnp.where(at >= k, turned[t], turned[t - 1]) for t in range(n)]
+
+    def read(f, r, h):
+        return [f[pl.ds(r, h), t * LANES : (t + 1) * LANES] for t in range(count_tiles)]
+
+    def write(f, r, x):
+        for t, v in enumerate(x):
+            f[pl.ds(r, v.shape[0]), t * LANES : (t + 1) * LANES] = v
+
+    every = range(count_tiles)
+
+    def first_step(r, h, n_before):
+        s, s_next = read(S, r, h), read(S, r + h, HALO)
+        m = read(M, r, h)
+        wet = [v + v for v in m]
+        e = from_right([v * w for v, w in zip(read(E, r, h), wet)], 1)
+        n0 = [v * w for v, w in zip(read(N, r, h), wet)]
+        m_next = read(M, r + h, HALO)
+        n_next = [v * (w + w) for v, w in zip(read(N, r + h, HALO), m_next)]
+        depth = read(CX, r, h)
+        cx = from_right(depth, 1)
+        cy = [below(v, w, 1) for v, w in zip(depth, read(CX, r + h, HALO))]
+        n = [below(v, w, 1) for v, w in zip(n0, n_next)]
+        s_right = from_right(s, 2)
+        e = [e[t] + cx[t] * (s_right[t] - s[t]) for t in every]
+        n = [n[t] + cy[t] * (below(s[t], s_next[t], 2) - s[t]) for t in every]
+        e_left = from_left(e, 2)
+        s = [m[t] * (s[t] + s[t] + ((e[t] - e_left[t]) + (n[t] - above(n_before[t], n[t], 2)))) for t in every]
+        for f, x in ((S, s), (E, e), (N, n), (CX, cx), (CY, cy)):
+            write(f, r, x)
+        return [v[h - HALO :] for v in n]
+
+    def second_step(r, h, n_before):
+        s, s_next = read(S, r, h), read(S, r + h, HALO)
+        e, n, m, cx, cy = (read(f, r, h) for f in (E, N, M, CX, CY))
+        s_right = from_right(s, 2)
+        e = [e[t] + cx[t] * (s_right[t] - s[t]) for t in every]
+        n = [n[t] + cy[t] * (below(s[t], s_next[t], 2) - s[t]) for t in every]
+        e_left = from_left(e, 2)
+        s = [s[t] + m[t] * ((e[t] - e_left[t]) + (n[t] - above(n_before[t], n[t], 2))) for t in every]
+        for f, x in ((S, s), (E, e), (N, n)):
+            write(f, r, x)
+        return [v[h - HALO :] for v in n]
+
+    within = (lax.broadcasted_iota(jnp.int32, (HALO, LANES), 0).astype(F32) + 0.5) / SPACING
+    lower = [spline_weight(within + 1.5 - m) for m in range(4)]
+    upper = [spline_weight(within + 1.0 - m) for m in range(4)]
+    mine_only = range(tiles)
+
+    def last_step(k, h, carry):
+        n_before, sums = carry
+        r = HALO + k
+        s, s_next = read(S, r, h), read(S, r + h, HALO)
+        e, n, m, cx, cy = (read(f, r, h) for f in (E, N, M, CX, CY))
+        s_right = from_right(s, 2)
+        e = [e[t] + cx[t] * (s_right[t] - s[t]) for t in every]
+        n = [n[t] + cy[t] * (below(s[t], s_next[t], 2) - s[t]) for t in mine_only]
+        e_left, e_own = from_left(e, 2), from_left(e, 1)
+        s = [s[t] + m[t] * ((e[t] - e_left[t]) + (n[t] - above(n_before[t], n[t], 2))) for t in mine_only]
+        write(s_out, k, s)
+        write(e_out, k, e_own[:tiles])
+        write(n_out, k, [above(n_before[t], n[t], 1) for t in mine_only])
+        sums = [list(x) for x in sums]
+        for q in range(h // SPACING):
+            done = []
+            for t in mine_only:
+                low = s[t][q * SPACING : q * SPACING + HALO]
+                up = s[t][q * SPACING + HALO : (q + 1) * SPACING]
+                a = [low * w for w in lower]
+                b = [up * w for w in upper]
+                c = sums[t]
+                done.append(jnp.sum(c[0] + a[0], axis=0, keepdims=True))
+                sums[t] = [c[1] + (a[1] + b[0]), c[2] + (a[2] + b[1]), c[3] + (a[3] + b[2]), b[3]]
+            R[pl.ds(k // SPACING + q, 1), :] = jnp.concatenate(done, axis=1)
+        return [v[h - HALO :] for v in n], sums
+
+    zero = [jnp.zeros((HALO, LANES), F32) for _ in every]
+    first_step(0, tall, zero)
+    second_step(0, tall, zero)
+    n_before = []
+    for t in mine_only:
+        span = slice(t * LANES, (t + 1) * LANES)
+        s = S[0:HALO, span]
+        n_before.append(N[0:HALO, span] + CY[0:HALO, span] * (below(s, S[HALO : 2 * HALO, span], 2) - s))
+    carry = (n_before, [[jnp.zeros((HALO, LANES), F32)] * 4 for _ in mine_only])
+
+    carry = last_step(0, rows, carry)
+    for k in range(4):
+        tail = [jnp.sum(carry[1][t][k], axis=0, keepdims=True) for t in mine_only]
+        R[rows // SPACING + k : rows // SPACING + k + 1, :] = jnp.concatenate(tail, axis=1)
 
     points = R.shape[0]
     stacked = jnp.concatenate([R[:, t * LANES : (t + 1) * LANES] for t in range(tiles)], axis=0)
@@ -322,6 +365,7 @@
     ]
     cross = messages(cross, len(rim) + len(side))
     start(cross)
+    points_load.wait()
     finish(cross)
 
     row = lax.broadcasted_iota(jnp.int32, (HALO, LANES), 0)
@@ -346,6 +390,15 @@
     grad[...] = inside * active[...].astype(F32) / SPACING
 
 
+def deliver(*refs):
+    sem = refs[8]
+    copies = [pltpu.make_async_copy(refs[k], refs[4 + k], sem.at[k]) for k in range(4)]
+    for copy in copies:
+        copy.start()
+    for copy in copies:
+        copy.wait()
+
+
 def local(surface_adjoint, east_adjoint, north_adjoint, water_depth, wet_mask, control_active):
     rows, cols = surface_adjoint.shape
     points = rows // SPACING + 4
@@ -356,32 +409,40 @@
     whole = pl.BlockSpec(memory_space=pltpu.VMEM)
     in_hbm = pl.BlockSpec(memory_space=pltpu.HBM)
     shape = jax.ShapeDtypeStruct((rows, cols), F32)
-    return pl.pallas_call(
+    hold = lambda x: pltpu.with_memory_space_constraint(x, pltpu.HBM)
+    s, e, n, g = pl.pallas_call(
         kernel,
         out_shape=(shape, shape, shape, jax.ShapeDtypeStruct(control_active.shape, F32)),
-        in_specs=[in_hbm] * 5 + [whole],
+        in_specs=[in_hbm] * 6,
         out_specs=(whole,) * 4,
         scratch_shapes=[
             field, field, field, field,
-            pltpu.VMEM((tall, wide), F32),
-            pltpu.VMEM((tall, wide), F32),
+            field, field,
             pltpu.VMEM((rows, cols), jnp.int32),
             pltpu.VMEM((points, cols), F32),
             pltpu.VMEM((points, LANES), F32),
+            pltpu.VMEM(control_active.shape, jnp.int32),
             pltpu.VMEM((quarter, LANES), F32),
             pltpu.VMEM((quarter, LANES), F32),
             pltpu.VMEM((quarter, LANES), F32),
             pltpu.VMEM((quarter, LANES), F32),
             pltpu.VMEM((4, HALO, LANES), F32),
             pltpu.VMEM((8, points, LANES), F32),
-            pltpu.SemaphoreType.DMA((25,)),
+            pltpu.SemaphoreType.DMA((26,)),
             pltpu.SemaphoreType.DMA((22,)),
             pltpu.SemaphoreType.DMA((22,)),
         ],
         compiler_params=pltpu.CompilerParams(
             collective_id=0, has_side_effects=True, vmem_limit_bytes=32 * 1024 * 1024
         ),
-    )(surface_adjoint, east_adjoint, north_adjoint, water_depth, wet_mask, control_active)
+    )(hold(surface_adjoint), hold(east_adjoint), hold(north_adjoint), hold(water_depth), hold(wet_mask), hold(control_active))
+    return pl.pallas_call(
+        deliver,
+        out_shape=(shape, shape, shape, jax.ShapeDtypeStruct(control_active.shape, F32)),
+        in_specs=[whole] * 4,
+        out_specs=(in_hbm,) * 4,
+        scratch_shapes=[pltpu.SemaphoreType.DMA((4,))],
+    )(*[pltpu.with_memory_space_constraint(x, pltpu.VMEM) for x in (s, e, n, g)])
 
 
 def solution(mesh):

time: 38.8 us -> 23.7 us (0.61)
  local copies, waits for them, and re-layouts: 10.3 us -> 0 us
  Pallas kernels: 27.5 us -> 23 us
    unnamed x16 -> x0, local copies, waits for them, and re-layouts: 10.3 us -> none
    pallas_call x1, Pallas kernels: 27.5 us -> 21.3 us  [local(): pl.pallas_call(kernel, out_shape=(shape, shape, shape, jax.ShapeDtypeStru...]
    pallas_call x0 -> x1, Pallas kernels: none -> 1.7 us  [local(): pl.pallas_call(deliver, out_shape=(shape, shape, shape, jax.ShapeDtypeStr...]
where the time goes in v2:
time: 23.7 us; the launch traced here: 23.6 us
  Pallas kernels  23 us (97%)
  between operations  0.64 us (3%)
    pallas_call x1, Pallas kernels, local(): pl.pallas_call(kernel, out_shape=(shape, shape, shape, jax.ShapeDtypeStru...  21.3 us
    pallas_call x1, Pallas kernels, local(): pl.pallas_call(deliver, out_shape=(shape, shape, shape, jax.ShapeDtypeStr...  1.7 us

profile of v2, /device:TPU:25, one launch (start us, length us, event | category | flops | bytes accessed | tf_op | source)
XLA Modules:
  0.0 23.6 jit_solution(5789199095552940954)
XLA Ops:
  0.6 21.3 %shard_map.93 = (f32[256,1024]{1,0:T(8,128)S(1)}, f32[256,1024]{1,0:T(8,128)S(1)}, f32[256,1024]{1,0:T(8,128)S(1)}, f32[16,64]{1,0:T(8,128)S(1)}) custom-call(f32[256,1024]{1,0:T(8,128)} %s_in.1, f32[256,1024]{1,0:T(8,128)} %e_in.1, f32[256,1024]{1,0:T(8,128)} %n_in.1, f32[256,1024]{1,0:T(8,128)} %d_in.1, s32[256,1024]{1,0:T(8,128)} %w_in.1, s32[16,64]{1,0:T(8,128)} %a_in.1), custom_call_target="tpu_custom_call" | custom-call | tf_op jit(solution)/shard_map/pallas_call | solution.py:413
  21.9 1.7 %shard_map.94 = (f32[256,1024]{1,0:T(8,128)}, f32[256,1024]{1,0:T(8,128)}, f32[256,1024]{1,0:T(8,128)}, f32[16,64]{1,0:T(8,128)}) custom-call(f32[256,1024]{1,0:T(8,128)S(1)} %get-tuple-element.8.refs_0_, f32[256,1024]{1,0:T(8,128)S(1)} %get-tuple-element.9.refs_1_, f32[256,1024]{1,0:T(8,128)S(1)} %get-tuple-element.10.refs_2_, ...), custom_call_target="tpu_custom_call" | custom-call | tf_op jit(solution)/shard_map/pallas_call | solution.py:439

commit v3 on v1

v3 whole, which is shorter than its diff:
```python
import jax
import jax.numpy as jnp
from jax import lax
from jax.experimental import pallas as pl
from jax.experimental.pallas import tpu as pltpu
from jax.sharding import PartitionSpec as P

SPACING = 16
LANES = 128
HALO = 8
STEPS = 3
F32 = jnp.float32

SOUTH, NORTH, WEST, EAST = (-1, 0), (1, 0), (0, -1), (0, 1)
SW, SE, NW, NE = (-1, -1), (-1, 1), (1, -1), (1, 1)
NEIGHBOURS = (SOUTH, NORTH, WEST, EAST, SW, SE, NW, NE)


def spline_weight(arg):
    mag = jnp.abs(arg)
    inner = 2.0 / 3.0 - mag * mag + 0.5 * mag * mag * mag
    outer = (2.0 - mag) * (2.0 - mag) * (2.0 - mag) / 6.0
    return jnp.where(mag < 1.0, inner, jnp.where(mag < 2.0, outer, 0.0 * mag))


def lanes_of(shape):
    return lax.broadcasted_iota(jnp.int32, shape, 1)


def below(x, following, k):
    return jnp.concatenate([x, following], axis=0)[k : k + x.shape[0]]


def above(preceding, x, k):
    return jnp.concatenate([preceding, x], axis=0)[HALO - k : HALO - k + x.shape[0]]


def turn(x, k):
    return pltpu.roll(x, k % LANES, axis=1) if k % LANES else x


def from_right(x, k):
    turned = [turn(v, -k) for v in x]
    if len(x) == 1:
        return turned
    at = lanes_of(x[0].shape)
    return [jnp.where(at < LANES - k, turned[t], turned[(t + 1) % len(x)]) for t in range(len(x))]


def from_left(x, k):
    turned = [turn(v, k) for v in x]
    if len(x) == 1:
        return turned
    at = lanes_of(x[0].shape)
    return [jnp.where(at >= k, turned[t], turned[t - 1]) for t in range(len(x))]


def up(x, k):
    none = jnp.zeros((HALO, LANES), F32)
    return [below(v, none, k) for v in x]


def down(x, k):
    none = jnp.zeros((HALO, LANES), F32)
    return [above(none, v, k) for v in x]


def change(s, e, n, cx, cy):
    s_right, s_up = from_right(s, 2), up(s, 2)
    e = [v + c * (r - o) for v, c, r, o in zip(e, cx, s_right, s)]
    n = [v + c * (r - o) for v, c, r, o in zip(n, cy, s_up, s)]
    flow = [(v - l) + (w - d) for v, l, w, d in zip(e, from_left(e, 2), n, down(n, 2))]
    return flow, e, n


def first_step(s, e, n, depth, m):
    wet = [v + v for v in m]
    e = from_right([v * w for v, w in zip(e, wet)], 1)
    n = up([v * w for v, w in zip(n, wet)], 1)
    cx, cy = from_right(depth, 1), up(depth, 1)
    flow, e, n = change(s, e, n, cx, cy)
    s = [w * (v + v + f) for w, v, f in zip(m, s, flow)]
    return s, e, n, cx, cy


def next_step(s, e, n, cx, cy, m):
    flow, e, n = change(s, e, n, cx, cy)
    return [v + w * f for v, w, f in zip(s, m, flow)], e, n


def march(s, e, n, depth):
    m = [jnp.where(v > 0.0, 0.5, 0.0) for v in depth]
    s, e, n, cx, cy = first_step(s, e, n, depth, m)
    for step in range(STEPS - 1):
        s, e, n = next_step(s, e, n, cx, cy, m)
    return s, from_left(e, 1), down(n, 1)


def kernel(
    s_in, e_in, n_in, d_in, w_in, a_in,
    s_out, e_out, n_out, grad,
    S, E, N, D, W, CY, M, R, PART, active,
    TOP, BOT, Z, pack_w, pack_e, got_w, got_e, corner, fold,
    load_sem, send_sem, recv_sem,
):
    rows, cols = s_out.shape
    tiles = cols // LANES
    quarter = rows // 4
    edge = 2 * HALO
    nlat, nlon = lax.axis_size("lat"), lax.axis_size("lon")
    lat, lon = lax.axis_index("lat"), lax.axis_index("lon")

    def has(offset):
        a, b = lat + offset[0], lon + offset[1]
        return (a >= 0) & (a < nlat) & (b >= 0) & (b < nlon)

    def opposite(offset):
        return (-offset[0], -offset[1])

    barrier = pltpu.get_barrier_semaphore()
    count = jnp.int32(0)
    for offset in NEIGHBOURS:
        count = count + has(offset).astype(jnp.int32)

        @pl.when(has(offset))
        def _(offset=offset):
            pl.semaphore_signal(
                barrier, inc=1,
                device_id={"lat": lat + offset[0], "lon": lon + offset[1]},
                device_id_type=pl.DeviceIdType.MESH,
            )

    regions = (
        (0, rows, 0, LANES),
        (0, rows, cols - LANES, LANES),
        (0, edge, LANES, cols - 2 * LANES),
        (rows - edge, edge, LANES, cols - 2 * LANES),
        (edge, rows - 2 * edge, LANES, cols - 2 * LANES),
    )
    loads = []
    for k, (r, h, c, w) in enumerate(regions):
        for a, (src, dst) in enumerate(((w_in, W), (d_in, D), (e_in, E), (n_in, N), (s_in, S))):
            loads.append(
                pltpu.make_async_copy(
                    src.at[pl.ds(r, h), pl.ds(c, w)],
                    dst.at[pl.ds(r, h), pl.ds(c, w)],
                    load_sem.at[k * 5 + a],
                )
            )
    loads.append(pltpu.make_async_copy(a_in, active, load_sem.at[25]))
    for copy in loads:
        copy.start()

    def messages(items, first):
        made = []
        for k, (src, dst, offset) in enumerate(items):
            made.append((
                pltpu.make_async_remote_copy(
                    src_ref=src, dst_ref=dst,
                    send_sem=send_sem.at[first + k], recv_sem=recv_sem.at[first + k],
                    device_id={"lat": lat + offset[0], "lon": lon + offset[1]},
                    device_id_type=pl.DeviceIdType.MESH,
                ),
                offset,
            ))
        return made

    def start(made):
        for copy, offset in made:
            @pl.when(has(offset))
            def _(copy=copy):
                copy.start()

    def finish(made):
        for copy, offset in made:
            @pl.when(has(opposite(offset)))
            def _(copy=copy):
                copy.wait_recv()

            @pl.when(has(offset))
            def _(copy=copy):
                copy.wait_send()

    every = pl.ds(0, 4)
    body = pl.ds(0, cols)
    halos = messages([
        (TOP.at[every, pl.ds(HALO, HALO), body], BOT.at[every, pl.ds(edge, HALO), body], SOUTH),
        (BOT.at[every, pl.ds(HALO, HALO), body], TOP.at[every, pl.ds(0, HALO), body], NORTH),
        (pack_w, got_e, WEST),
        (pack_e, got_w, EAST),
        (pack_w.at[pl.ds(0, HALO)], corner.at[3], SW),
        (pack_e.at[pl.ds(0, HALO)], corner.at[2], SE),
        (pack_w.at[pl.ds(quarter - HALO, HALO)], corner.at[1], NW),
        (pack_e.at[pl.ds(quarter - HALO, HALO)], corner.at[0], NE),
    ], 0)

    @pl.when(lat == 0)
    def _():
        TOP[:, 0:HALO, 0:cols] = jnp.zeros((4, HALO, cols), F32)
        fold[0] = jnp.zeros_like(fold[0])

    @pl.when(lat == nlat - 1)
    def _():
        BOT[:, edge : edge + HALO, 0:cols] = jnp.zeros((4, HALO, cols), F32)
        fold[1] = jnp.zeros_like(fold[1])

    for pack, offset, k in ((got_w, WEST, 2), (got_e, EAST, 3)):
        @pl.when(jnp.logical_not(has(offset)))
        def _(pack=pack, k=k):
            pack[...] = jnp.zeros_like(pack)
            fold[k] = jnp.zeros_like(fold[k])

    for k, offset in enumerate((SW, SE, NW, NE)):
        @pl.when(jnp.logical_not(has(offset)))
        def _(k=k):
            corner[k] = jnp.zeros_like(corner[k])
            fold[4 + k] = jnp.zeros_like(fold[4 + k])

    R[...] = jnp.zeros_like(R)

    def span(t):
        return slice(t * LANES, (t + 1) * LANES)

    def cell(f, r, h, t):
        return f[r : r + h, span(t)]

    def depth_of(r, h, t):
        return cell(D, r, h, t) * (0.5 * cell(W, r, h, t).astype(F32))

    for copy in loads[:20]:
        copy.wait()

    lane = lanes_of((quarter, LANES))
    far = tiles - 1
    sides = {}
    for t in (0, far):
        sides[t] = [cell(f, 0, rows, t) for f in (S, E, N)] + [depth_of(0, rows, t)]
    for pack, t, extra in ((pack_w, 0, 0), (pack_e, far, 1)):
        total = jnp.zeros((quarter, LANES), F32)
        for a in range(4):
            for b in range(4):
                g = 4 * b + a
                piece = turn(sides[t][a][b * quarter : (b + 1) * quarter], 8 * (g + extra))
                total = jnp.where((lane >= 8 * g) & (lane < 8 * g + 8), piece, total)
        pack[...] = total
    for a, f in enumerate((S, E, N, None)):
        for t in range(tiles):
            for buffer, to, r in ((TOP, HALO, 0), (BOT, 0, rows - edge)):
                v = depth_of(r, edge, t) if f is None else cell(f, r, edge, t)
                buffer[a, to : to + edge, span(t)] = v

    tall_lane = lanes_of((rows, LANES))
    for a in range(4):
        Z[a] = jnp.where(tall_lane < 56, turn(sides[far][a], 56), jnp.where(tall_lane >= 72, turn(sides[0][a], 72), 0.0))

    for copy in loads[20:]:
        copy.wait()

    def read(f):
        return [cell(f, 0, rows, t) for t in range(tiles)]

    def write(f, x):
        for t, v in enumerate(x):
            f[:, span(t)] = v

    m = [0.5 * v.astype(F32) for v in read(W)]
    depth = [v * w for v, w in zip(read(D), m)]
    s, e, n, cx, cy = first_step(read(S), read(E), read(N), depth, m)
    for f, x in ((S, s), (E, e), (N, n), (D, cx), (CY, cy), (M, m)):
        write(f, x)

    pl.semaphore_wait(barrier, count)
    start(halos)

    for step in range(STEPS - 2):
        s, e, n = next_step(*(read(f) for f in (S, E, N, D, CY, M)))
        for f, x in ((S, s), (E, e), (N, n)):
            write(f, x)

    s, e, n = next_step(*(read(f) for f in (S, E, N, D, CY, M)))
    for f, x in ((s_out, s), (e_out, from_left(e, 1)), (n_out, down(n, 1))):
        write(f, x)

    within = (lax.broadcasted_iota(jnp.int32, (HALO, LANES), 0).astype(F32) + 0.5) / SPACING
    lower = [spline_weight(within + 1.5 - k) for k in range(4)]
    upper = [spline_weight(within + 1.0 - k) for k in range(4)]

    def total_of(x):
        return jnp.sum(x, axis=0, keepdims=True)

    def row_sums(v, t):
        none = jnp.zeros((HALO, LANES), F32)
        c = [none] * 4
        cells = rows // SPACING
        for q in range(cells):
            r = q * SPACING
            low, high = v[r : r + HALO], v[r + HALO : r + SPACING]
            a = [none] * 4 if q == 0 else [low * w for w in lower]
            b = [none] * 4 if q == cells - 1 else [high * w for w in upper]
            R[q : q + 1, span(t)] = total_of(c[0] + a[0])
            c = [c[1] + (a[1] + b[0]), c[2] + (a[2] + b[1]), c[3] + (a[3] + b[2]), b[3]]
        for k in range(4):
            R[cells + k : cells + k + 1, span(t)] = total_of(c[k])

    s[0] = jnp.where(tall_lane >= 8, s[0], 0.0)
    s[far] = jnp.where(tall_lane < LANES - 8, s[far], 0.0)
    for t in range(tiles):
        row_sums(s[t], t)

    shape = (LANES, LANES)
    at = lax.broadcasted_iota(jnp.int32, shape, 0)
    point = lanes_of(shape).astype(F32) - 2.0 + 0.5
    column_weight = spline_weight((at.astype(F32) + 0.5) / SPACING - point)
    strip_column = jnp.where(at < 64, at + (cols - 56), at - 72)
    strip_weight = spline_weight((strip_column.astype(F32) + 0.5) / SPACING - point)
    strip_weight = jnp.where(((at >= 48) & (at < 56)) | ((at >= 72) & (at < 80)), strip_weight, 0.0)

    finish(halos)

    def ring(east, west, g):
        x = lanes_of(east.shape)
        return jnp.where(x < 8, turn(east, -8 * g), jnp.where(x >= LANES - 8, turn(west, -8 * (g + 1)), 0.0))

    edges = []
    for buffer in (TOP, BOT):
        fields = []
        for a in range(4):
            if buffer is TOP:
                parts = [ring(corner[1], corner[0], 12 + a), ring(got_e[0:edge], got_w[0:edge], a)]
            else:
                last = slice(quarter - edge, quarter)
                parts = [ring(got_e[last], got_w[last], 12 + a), ring(corner[3], corner[2], a)]
            fields.append([buffer[a, :, span(t)] for t in range(tiles)] + [jnp.concatenate(parts, axis=0)])
        edges.append(march(*fields))

    fields = []
    for a in range(4):
        parts = []
        for b in range(4):
            g = 4 * b + a
            own = Z[a, b * quarter : (b + 1) * quarter]
            own = jnp.where((lane >= 56) & (lane < 64), turn(got_e[...], 56 - 8 * g), own)
            parts.append(jnp.where((lane >= 64) & (lane < 72), turn(got_w[...], 64 - 8 * g), own))
        fields.append([jnp.concatenate(parts, axis=0)])
    strip = march(*fields)

    middle = slice(HALO, rows - HALO)
    for f, z, south, north in zip((s_out, e_out, n_out), strip, *edges):
        x = lanes_of((rows - 2 * HALO, LANES))
        f[middle, span(0)] = jnp.where(x < 8, turn(z[0][middle], -72), f[middle, span(0)])
        f[middle, span(far)] = jnp.where(x >= LANES - 8, turn(z[0][middle], 72), f[middle, span(far)])
        for t in range(tiles):
            f[0:HALO, span(t)] = south[t][HALO:edge]
            f[rows - HALO : rows, span(t)] = north[t][HALO:edge]

    row_sums(strip[0][0], tiles)
    cells = rows // SPACING
    for t in range(tiles):
        south, north = edges[0][0][t][HALO:edge], edges[1][0][t][HALO:edge]
        for k in range(4):
            R[k : k + 1, span(t)] += total_of(south * lower[k])
            R[cells + k : cells + k + 1, span(t)] += total_of(north * upper[k])

    points = R.shape[0]

    def dot(x, w):
        return jnp.dot(x, w, precision=lax.Precision.HIGHEST, preferred_element_type=F32)

    spread = dot(jnp.concatenate([R[:, span(t)] for t in range(tiles)], axis=0), column_weight)
    own = dot(R[:, span(tiles)], strip_weight)
    for t in range(tiles):
        own = own + turn(spread[t * points : (t + 1) * points], 8 * t)
    PART[...] = own

    top, bottom = pl.ds(0, HALO), pl.ds(points - HALO, HALO)
    cross = [
        (PART.at[bottom], fold.at[0, top], NORTH),
        (PART.at[top], fold.at[1, top], SOUTH),
        (PART, fold.at[2], EAST),
        (PART, fold.at[3], WEST),
        (PART.at[bottom], fold.at[4, top], NE),
        (PART.at[bottom], fold.at[5, top], NW),
        (PART.at[top], fold.at[6, top], SE),
        (PART.at[top], fold.at[7, top], SW),
    ]
    cross = messages(cross, len(halos))
    start(cross)
    finish(cross)

    row = lax.broadcasted_iota(jnp.int32, (HALO, LANES), 0)
    lane = lanes_of((points, LANES))

    def with_rows(middle, south, north):
        south = jnp.where((row == 2) | (row == 3), south, 0.0)
        north = jnp.where(row < 2, north, 0.0)
        return jnp.concatenate(
            [middle[:HALO] + south, middle[HALO : points - HALO], middle[points - HALO :] + north], axis=0
        )

    mine = with_rows(own, fold[0, 0:HALO], fold[1, 0:HALO])
    west = with_rows(fold[2], fold[4, 0:HALO], fold[6, 0:HALO])
    east = with_rows(fold[3], fold[5, 0:HALO], fold[7, 0:HALO])
    half = cols // SPACING
    west = turn(west, -half)
    east = turn(east, half)
    mine = mine + jnp.where((lane == 2) | (lane == 3), west, 0.0)
    mine = mine + jnp.where((lane == half) | (lane == half + 1), east, 0.0)
    inside = mine[2 : 2 + rows // SPACING, 2 : 2 + half]
    grad[...] = inside * active[...].astype(F32) / SPACING


def deliver(*refs):
    sem = refs[8]
    copies = [pltpu.make_async_copy(refs[k], refs[4 + k], sem.at[k]) for k in range(4)]
    for copy in copies:
        copy.start()
    for copy in copies:
        copy.wait()


def local(surface_adjoint, east_adjoint, north_adjoint, water_depth, wet_mask, control_active):
    rows, cols = surface_adjoint.shape
    points = rows // SPACING + 4
    points = (points + 7) // 8 * 8
    field = pltpu.VMEM((rows, cols), F32)
    rim = pltpu.VMEM((4, 3 * HALO, cols), F32)
    pack = pltpu.VMEM((rows // 4, LANES), F32)
    whole = pl.BlockSpec(memory_space=pltpu.VMEM)
    in_hbm = pl.BlockSpec(memory_space=pltpu.HBM)
    shape = jax.ShapeDtypeStruct((rows, cols), F32)
    hold = lambda x: pltpu.with_memory_space_constraint(x, pltpu.HBM)
    s, e, n, g = pl.pallas_call(
        kernel,
        out_shape=(shape, shape, shape, jax.ShapeDtypeStruct(control_active.shape, F32)),
        in_specs=[in_hbm] * 6,
        out_specs=(whole,) * 4,
        scratch_shapes=[
            field, field, field, field,
            pltpu.VMEM((rows, cols), jnp.int32),
            field, field,
            pltpu.VMEM((points, cols + LANES), F32),
            pltpu.VMEM((points, LANES), F32),
            pltpu.VMEM(control_active.shape, jnp.int32),
            rim, rim,
            pltpu.VMEM((4, rows, LANES), F32),
            pack, pack, pack, pack,
            pltpu.VMEM((4, HALO, LANES), F32),
            pltpu.VMEM((8, points, LANES), F32),
            pltpu.SemaphoreType.DMA((26,)),
            pltpu.SemaphoreType.DMA((16,)),
            pltpu.SemaphoreType.DMA((16,)),
        ],
        compiler_params=pltpu.CompilerParams(
            collective_id=0, has_side_effects=True, vmem_limit_bytes=32 * 1024 * 1024
        ),
    )(hold(surface_adjoint), hold(east_adjoint), hold(north_adjoint), hold(water_depth), hold(wet_mask), hold(control_active))
    return pl.pallas_call(
        deliver,
        out_shape=(shape, shape, shape, jax.ShapeDtypeStruct(control_active.shape, F32)),
        in_specs=[whole] * 4,
        out_specs=(in_hbm,) * 4,
        scratch_shapes=[pltpu.SemaphoreType.DMA((4,))],
    )(*[pltpu.with_memory_space_constraint(x, pltpu.VMEM) for x in (s, e, n, g)])


def solution(mesh):
    spec = P("lat", "lon")
    return jax.shard_map(
        local, mesh=mesh, in_specs=(spec,) * 6, out_specs=(spec,) * 4, check_vma=False
    )
```

time: 38.8 us -> 21.7 us (0.56)
  local copies, waits for them, and re-layouts: 10.3 us -> 0 us
  Pallas kernels: 27.5 us -> 20.9 us
    unnamed x16 -> x0, local copies, waits for them, and re-layouts: 10.3 us -> none
    pallas_call x1, Pallas kernels: 27.5 us -> 19.2 us  [local(): pl.pallas_call(kernel, out_shape=(shape, shape, shape, jax.ShapeDtypeStru...]
    pallas_call x0 -> x1, Pallas kernels: none -> 1.7 us  [local(): pl.pallas_call(deliver, out_shape=(shape, shape, shape, jax.ShapeDtypeStr...]
where the time goes in v3:
time: 21.7 us; the launch traced here: 21.6 us
  Pallas kernels  20.9 us (96%)
  between operations  0.64 us (3%)
    pallas_call x1, Pallas kernels, local(): pl.pallas_call(kernel, out_shape=(shape, shape, shape, jax.ShapeDtypeStru...  19.2 us
    pallas_call x1, Pallas kernels, local(): pl.pallas_call(deliver, out_shape=(shape, shape, shape, jax.ShapeDtypeStr...  1.7 us

profile of v3, /device:TPU:25, one launch (start us, length us, event | category | flops | bytes accessed | tf_op | source)
XLA Modules:
  0.0 21.6 jit_solution(7097106244068959215)
XLA Ops:
  0.6 19.2 %shard_map.93 = (f32[256,1024]{1,0:T(8,128)S(1)}, f32[256,1024]{1,0:T(8,128)S(1)}, f32[256,1024]{1,0:T(8,128)S(1)}, f32[16,64]{1,0:T(8,128)S(1)}) custom-call(f32[256,1024]{1,0:T(8,128)} %s_in.1, f32[256,1024]{1,0:T(8,128)} %e_in.1, f32[256,1024]{1,0:T(8,128)} %n_in.1, f32[256,1024]{1,0:T(8,128)} %d_in.1, s32[256,1024]{1,0:T(8,128)} %w_in.1, s32[16,64]{1,0:T(8,128)} %a_in.1), custom_call_target="tpu_custom_call" | custom-call | tf_op jit(solution)/shard_map/pallas_call | solution.py:432
  19.9 1.7 %shard_map.94 = (f32[256,1024]{1,0:T(8,128)}, f32[256,1024]{1,0:T(8,128)}, f32[256,1024]{1,0:T(8,128)}, f32[16,64]{1,0:T(8,128)}) custom-call(f32[256,1024]{1,0:T(8,128)S(1)} %get-tuple-element.8.refs_0_, f32[256,1024]{1,0:T(8,128)S(1)} %get-tuple-element.9.refs_1_, f32[256,1024]{1,0:T(8,128)S(1)} %get-tuple-element.10.refs_2_, ...), custom_call_target="tpu_custom_call" | custom-call | tf_op jit(solution)/shard_map/pallas_call | solution.py:457

commit v4 on v3

--- a/solution.py
+++ b/solution.py
@@ -8,6 +8,7 @@
 SPACING = 16
 LANES = 128
 HALO = 8
+WIDE = 32
 STEPS = 3
 F32 = jnp.float32
 
@@ -105,7 +106,6 @@
 ):
     rows, cols = s_out.shape
     tiles = cols // LANES
-    quarter = rows // 4
     edge = 2 * HALO
     nlat, nlon = lax.axis_size("lat"), lax.axis_size("lon")
     lat, lon = lax.axis_index("lat"), lax.axis_index("lon")
@@ -190,8 +190,8 @@
         (pack_e, got_w, EAST),
         (pack_w.at[pl.ds(0, HALO)], corner.at[3], SW),
         (pack_e.at[pl.ds(0, HALO)], corner.at[2], SE),
-        (pack_w.at[pl.ds(quarter - HALO, HALO)], corner.at[1], NW),
-        (pack_e.at[pl.ds(quarter - HALO, HALO)], corner.at[0], NE),
+        (pack_w.at[pl.ds(rows - HALO, HALO)], corner.at[1], NW),
+        (pack_e.at[pl.ds(rows - HALO, HALO)], corner.at[0], NE),
     ], 0)
 
     @pl.when(lat == 0)
@@ -204,17 +204,15 @@
         BOT[:, edge : edge + HALO, 0:cols] = jnp.zeros((4, HALO, cols), F32)
         fold[1] = jnp.zeros_like(fold[1])
 
-    for pack, offset, k in ((got_w, WEST, 2), (got_e, EAST, 3)):
+    for pack, offset in ((got_w, WEST), (got_e, EAST)):
         @pl.when(jnp.logical_not(has(offset)))
-        def _(pack=pack, k=k):
+        def _(pack=pack):
             pack[...] = jnp.zeros_like(pack)
-            fold[k] = jnp.zeros_like(fold[k])
 
     for k, offset in enumerate((SW, SE, NW, NE)):
         @pl.when(jnp.logical_not(has(offset)))
         def _(k=k):
             corner[k] = jnp.zeros_like(corner[k])
-            fold[4 + k] = jnp.zeros_like(fold[4 + k])
 
     R[...] = jnp.zeros_like(R)
 
@@ -230,28 +228,31 @@
     for copy in loads[:20]:
         copy.wait()
 
-    lane = lanes_of((quarter, LANES))
+    lane = lanes_of((rows, LANES))
     far = tiles - 1
     sides = {}
     for t in (0, far):
         sides[t] = [cell(f, 0, rows, t) for f in (S, E, N)] + [depth_of(0, rows, t)]
-    for pack, t, extra in ((pack_w, 0, 0), (pack_e, far, 1)):
-        total = jnp.zeros((quarter, LANES), F32)
-        for a in range(4):
-            for b in range(4):
-                g = 4 * b + a
-                piece = turn(sides[t][a][b * quarter : (b + 1) * quarter], 8 * (g + extra))
-                total = jnp.where((lane >= 8 * g) & (lane < 8 * g + 8), piece, total)
-        pack[...] = total
+
+    def pick(x, pieces):
+        total = pieces[-1]
+        for k in (2, 1, 0):
+            total = jnp.where(x < WIDE * (k + 1), pieces[k], total)
+        return total
+
+    pack_w[...] = pick(lane, [turn(sides[0][a], WIDE * a) for a in range(4)])
+    pack_e[...] = pick(lane, [turn(sides[far][a], WIDE * (a + 1)) for a in range(4)])
     for a, f in enumerate((S, E, N, None)):
         for t in range(tiles):
             for buffer, to, r in ((TOP, HALO, 0), (BOT, 0, rows - edge)):
                 v = depth_of(r, edge, t) if f is None else cell(f, r, edge, t)
                 buffer[a, to : to + edge, span(t)] = v
 
-    tall_lane = lanes_of((rows, LANES))
+    pl.semaphore_wait(barrier, count)
+    start(halos)
+
     for a in range(4):
-        Z[a] = jnp.where(tall_lane < 56, turn(sides[far][a], 56), jnp.where(tall_lane >= 72, turn(sides[0][a], 72), 0.0))
+        Z[a] = jnp.where(lane < 64, turn(sides[far][a], WIDE), turn(sides[0][a], -WIDE))
 
     for copy in loads[20:]:
         copy.wait()
@@ -268,9 +269,6 @@
     s, e, n, cx, cy = first_step(read(S), read(E), read(N), depth, m)
     for f, x in ((S, s), (E, e), (N, n), (D, cx), (CY, cy), (M, m)):
         write(f, x)
-
-    pl.semaphore_wait(barrier, count)
-    start(halos)
 
     for step in range(STEPS - 2):
         s, e, n = next_step(*(read(f) for f in (S, E, N, D, CY, M)))
@@ -302,8 +300,8 @@
         for k in range(4):
             R[cells + k : cells + k + 1, span(t)] = total_of(c[k])
 
-    s[0] = jnp.where(tall_lane >= 8, s[0], 0.0)
-    s[far] = jnp.where(tall_lane < LANES - 8, s[far], 0.0)
+    s[0] = jnp.where(lane >= 8, s[0], 0.0)
+    s[far] = jnp.where(lane < LANES - 8, s[far], 0.0)
     for t in range(tiles):
         row_sums(s[t], t)
 
@@ -311,52 +309,57 @@
     at = lax.broadcasted_iota(jnp.int32, shape, 0)
     point = lanes_of(shape).astype(F32) - 2.0 + 0.5
     column_weight = spline_weight((at.astype(F32) + 0.5) / SPACING - point)
-    strip_column = jnp.where(at < 64, at + (cols - 56), at - 72)
+    strip_column = jnp.where(at < 64, at + (cols - WIDE), at - 3 * WIDE)
     strip_weight = spline_weight((strip_column.astype(F32) + 0.5) / SPACING - point)
-    strip_weight = jnp.where(((at >= 48) & (at < 56)) | ((at >= 72) & (at < 80)), strip_weight, 0.0)
+    strip_weight = jnp.where((at >= WIDE - 8) & (at < 3 * WIDE + 8), strip_weight, 0.0)
 
     finish(halos)
 
-    def ring(east, west, g):
+    def ring(east, west, a):
         x = lanes_of(east.shape)
-        return jnp.where(x < 8, turn(east, -8 * g), jnp.where(x >= LANES - 8, turn(west, -8 * (g + 1)), 0.0))
+        east, west = turn(east, -WIDE * a), turn(west, -WIDE * (a + 1))
+        return jnp.where(x < WIDE, east, jnp.where(x >= LANES - WIDE, west, 0.0))
 
     edges = []
     for buffer in (TOP, BOT):
         fields = []
         for a in range(4):
             if buffer is TOP:
-                parts = [ring(corner[1], corner[0], 12 + a), ring(got_e[0:edge], got_w[0:edge], a)]
+                parts = [ring(corner[1], corner[0], a), ring(got_e[0:edge], got_w[0:edge], a)]
             else:
-                last = slice(quarter - edge, quarter)
-                parts = [ring(got_e[last], got_w[last], 12 + a), ring(corner[3], corner[2], a)]
+                last = slice(rows - edge, rows)
+                parts = [ring(got_e[last], got_w[last], a), ring(corner[3], corner[2], a)]
             fields.append([buffer[a, :, span(t)] for t in range(tiles)] + [jnp.concatenate(parts, axis=0)])
         edges.append(march(*fields))
 
     fields = []
     for a in range(4):
-        parts = []
-        for b in range(4):
-            g = 4 * b + a
-            own = Z[a, b * quarter : (b + 1) * quarter]
-            own = jnp.where((lane >= 56) & (lane < 64), turn(got_e[...], 56 - 8 * g), own)
-            parts.append(jnp.where((lane >= 64) & (lane < 72), turn(got_w[...], 64 - 8 * g), own))
-        fields.append([jnp.concatenate(parts, axis=0)])
+        own = Z[a]
+        pieces = [own, turn(got_e[...], WIDE * (1 - a)), turn(got_w[...], WIDE * (2 - a)), own]
+        fields.append([pick(lane, pieces)])
     strip = march(*fields)
 
     middle = slice(HALO, rows - HALO)
     for f, z, south, north in zip((s_out, e_out, n_out), strip, *edges):
         x = lanes_of((rows - 2 * HALO, LANES))
-        f[middle, span(0)] = jnp.where(x < 8, turn(z[0][middle], -72), f[middle, span(0)])
-        f[middle, span(far)] = jnp.where(x >= LANES - 8, turn(z[0][middle], 72), f[middle, span(far)])
+        f[middle, span(0)] = jnp.where(x < 8, turn(z[0][middle], WIDE), f[middle, span(0)])
+        f[middle, span(far)] = jnp.where(x >= LANES - 8, turn(z[0][middle], -WIDE), f[middle, span(far)])
         for t in range(tiles):
             f[0:HALO, span(t)] = south[t][HALO:edge]
             f[rows - HALO : rows, span(t)] = north[t][HALO:edge]
 
     row_sums(strip[0][0], tiles)
     cells = rows // SPACING
-    for t in range(tiles):
+
+    def beyond(x):
+        at = lanes_of(x.shape)
+        x = jnp.where(at < 64, turn(x, WIDE), turn(x, -WIDE))
+        return jnp.where((at >= WIDE) & (at < 3 * WIDE), x, 0.0)
+
+    for t in range(tiles + 1):
         south, north = edges[0][0][t][HALO:edge], edges[1][0][t][HALO:edge]
+        if t == tiles:
+            south, north = beyond(south), beyond(north)
         for k in range(4):
             R[k : k + 1, span(t)] += total_of(south * lower[k])
             R[cells + k : cells + k + 1, span(t)] += total_of(north * upper[k])
@@ -373,39 +376,20 @@
     PART[...] = own
 
     top, bottom = pl.ds(0, HALO), pl.ds(points - HALO, HALO)
-    cross = [
-        (PART.at[bottom], fold.at[0, top], NORTH),
-        (PART.at[top], fold.at[1, top], SOUTH),
-        (PART, fold.at[2], EAST),
-        (PART, fold.at[3], WEST),
-        (PART.at[bottom], fold.at[4, top], NE),
-        (PART.at[bottom], fold.at[5, top], NW),
-        (PART.at[top], fold.at[6, top], SE),
-        (PART.at[top], fold.at[7, top], SW),
-    ]
-    cross = messages(cross, len(halos))
+    cross = messages([
+        (PART.at[bottom], fold.at[0], NORTH),
+        (PART.at[top], fold.at[1], SOUTH),
+    ], len(halos))
     start(cross)
     finish(cross)
 
     row = lax.broadcasted_iota(jnp.int32, (HALO, LANES), 0)
-    lane = lanes_of((points, LANES))
-
-    def with_rows(middle, south, north):
-        south = jnp.where((row == 2) | (row == 3), south, 0.0)
-        north = jnp.where(row < 2, north, 0.0)
-        return jnp.concatenate(
-            [middle[:HALO] + south, middle[HALO : points - HALO], middle[points - HALO :] + north], axis=0
-        )
-
-    mine = with_rows(own, fold[0, 0:HALO], fold[1, 0:HALO])
-    west = with_rows(fold[2], fold[4, 0:HALO], fold[6, 0:HALO])
-    east = with_rows(fold[3], fold[5, 0:HALO], fold[7, 0:HALO])
-    half = cols // SPACING
-    west = turn(west, -half)
-    east = turn(east, half)
-    mine = mine + jnp.where((lane == 2) | (lane == 3), west, 0.0)
-    mine = mine + jnp.where((lane == half) | (lane == half + 1), east, 0.0)
-    inside = mine[2 : 2 + rows // SPACING, 2 : 2 + half]
+    mine = jnp.concatenate([
+        own[:HALO] + jnp.where((row == 2) | (row == 3), fold[0], 0.0),
+        own[HALO : points - HALO],
+        own[points - HALO :] + jnp.where(row < 2, fold[1], 0.0),
+    ], axis=0)
+    inside = mine[2 : 2 + rows // SPACING, 2 : 2 + cols // SPACING]
     grad[...] = inside * active[...].astype(F32) / SPACING
 
 
@@ -424,7 +408,7 @@
     points = (points + 7) // 8 * 8
     field = pltpu.VMEM((rows, cols), F32)
     rim = pltpu.VMEM((4, 3 * HALO, cols), F32)
-    pack = pltpu.VMEM((rows // 4, LANES), F32)
+    pack = pltpu.VMEM((rows, LANES), F32)
     whole = pl.BlockSpec(memory_space=pltpu.VMEM)
     in_hbm = pl.BlockSpec(memory_space=pltpu.HBM)
     shape = jax.ShapeDtypeStruct((rows, cols), F32)
@@ -445,10 +429,10 @@
             pltpu.VMEM((4, rows, LANES), F32),
             pack, pack, pack, pack,
             pltpu.VMEM((4, HALO, LANES), F32),
-            pltpu.VMEM((8, points, LANES), F32),
+            pltpu.VMEM((2, HALO, LANES), F32),
             pltpu.SemaphoreType.DMA((26,)),
-            pltpu.SemaphoreType.DMA((16,)),
-            pltpu.SemaphoreType.DMA((16,)),
+            pltpu.SemaphoreType.DMA((10,)),
+            pltpu.SemaphoreType.DMA((10,)),
         ],
         compiler_params=pltpu.CompilerParams(
             collective_id=0, has_side_effects=True, vmem_limit_bytes=32 * 1024 * 1024

time: 21.7 us -> 20.3 us (0.935)
  Pallas kernels: 20.9 us -> 19.6 us
    pallas_call x1, Pallas kernels: 19.2 us -> 17.9 us  [local(): pl.pallas_call(kernel, out_shape=(shape, shape, shape, jax.ShapeDtypeStru...]
where the time goes in v4:
time: 20.3 us; the launch traced here: 20.2 us
  Pallas kernels  19.6 us (97%)
  between operations  0.64 us (3%)
    pallas_call x1, Pallas kernels, local(): pl.pallas_call(kernel, out_shape=(shape, shape, shape, jax.ShapeDtypeStru...  17.9 us
    pallas_call x1, Pallas kernels, local(): pl.pallas_call(deliver, out_shape=(shape, shape, shape, jax.ShapeDtypeStr...  1.7 us

profile of v4, /device:TPU:25, one launch (start us, length us, event | category | flops | bytes accessed | tf_op | source)
XLA Modules:
  0.0 20.2 jit_solution(3888908838990077864)
XLA Ops:
  0.6 17.9 %shard_map.93 = (f32[256,1024]{1,0:T(8,128)S(1)}, f32[256,1024]{1,0:T(8,128)S(1)}, f32[256,1024]{1,0:T(8,128)S(1)}, f32[16,64]{1,0:T(8,128)S(1)}) custom-call(f32[256,1024]{1,0:T(8,128)} %s_in.1, f32[256,1024]{1,0:T(8,128)} %e_in.1, f32[256,1024]{1,0:T(8,128)} %n_in.1, f32[256,1024]{1,0:T(8,128)} %d_in.1, s32[256,1024]{1,0:T(8,128)} %w_in.1, s32[16,64]{1,0:T(8,128)} %a_in.1), custom_call_target="tpu_custom_call" | custom-call | tf_op jit(solution)/shard_map/pallas_call | solution.py:416
  18.5 1.7 %shard_map.94 = (f32[256,1024]{1,0:T(8,128)}, f32[256,1024]{1,0:T(8,128)}, f32[256,1024]{1,0:T(8,128)}, f32[16,64]{1,0:T(8,128)}) custom-call(f32[256,1024]{1,0:T(8,128)S(1)} %get-tuple-element.8.refs_0_, f32[256,1024]{1,0:T(8,128)S(1)} %get-tuple-element.9.refs_1_, f32[256,1024]{1,0:T(8,128)S(1)} %get-tuple-element.10.refs_2_, ...), custom_call_target="tpu_custom_call" | custom-call | tf_op jit(solution)/shard_map/pallas_call | solution.py:441

commit v5 on v4

--- a/solution.py
+++ b/solution.py
@@ -9,6 +9,8 @@
 LANES = 128
 HALO = 8
 WIDE = 32
+CHUNKS = 4
+PIECES = 1
 STEPS = 3
 F32 = jnp.float32
 
@@ -56,30 +58,31 @@
     return [jnp.where(at >= k, turned[t], turned[t - 1]) for t in range(len(x))]
 
 
-def up(x, k):
+def up(x, k, following=None):
     none = jnp.zeros((HALO, LANES), F32)
-    return [below(v, none, k) for v in x]
-
-
-def down(x, k):
+    return [below(v, following[i] if following else none, k) for i, v in enumerate(x)]
+
+
+def down(x, k, preceding=None):
     none = jnp.zeros((HALO, LANES), F32)
-    return [above(none, v, k) for v in x]
-
-
-def change(s, e, n, cx, cy):
-    s_right, s_up = from_right(s, 2), up(s, 2)
+    return [above(preceding[i] if preceding else none, v, k) for i, v in enumerate(x)]
+
+
+def change(s, e, n, cx, cy, s_after=None, n_before=None):
+    s_right, s_up = from_right(s, 2), up(s, 2, s_after)
     e = [v + c * (r - o) for v, c, r, o in zip(e, cx, s_right, s)]
     n = [v + c * (r - o) for v, c, r, o in zip(n, cy, s_up, s)]
-    flow = [(v - l) + (w - d) for v, l, w, d in zip(e, from_left(e, 2), n, down(n, 2))]
+    flow = [(v - l) + (w - d) for v, l, w, d in zip(e, from_left(e, 2), n, down(n, 2, n_before))]
     return flow, e, n
 
 
-def first_step(s, e, n, depth, m):
+def first_step(s, e, n, depth, m, after=(None, None, None), n_before=None):
+    s_after, n_after, depth_after = after
     wet = [v + v for v in m]
     e = from_right([v * w for v, w in zip(e, wet)], 1)
-    n = up([v * w for v, w in zip(n, wet)], 1)
-    cx, cy = from_right(depth, 1), up(depth, 1)
-    flow, e, n = change(s, e, n, cx, cy)
+    n = up([v * w for v, w in zip(n, wet)], 1, n_after)
+    cx, cy = from_right(depth, 1), up(depth, 1, depth_after)
+    flow, e, n = change(s, e, n, cx, cy, s_after, n_before)
     s = [w * (v + v + f) for w, v, f in zip(m, s, flow)]
     return s, e, n, cx, cy
 
@@ -130,13 +133,15 @@
                 device_id_type=pl.DeviceIdType.MESH,
             )
 
+    part = (rows - 2 * edge) // (HALO * CHUNKS) * HALO
+    chunks = [(edge + k * part, part) for k in range(CHUNKS - 1)]
+    chunks.append((edge + (CHUNKS - 1) * part, rows - 2 * edge - (CHUNKS - 1) * part))
     regions = (
         (0, rows, 0, LANES),
         (0, rows, cols - LANES, LANES),
         (0, edge, LANES, cols - 2 * LANES),
         (rows - edge, edge, LANES, cols - 2 * LANES),
-        (edge, rows - 2 * edge, LANES, cols - 2 * LANES),
-    )
+    ) + tuple((r, h, LANES, cols - 2 * LANES) for r, h in chunks)
     loads = []
     for k, (r, h, c, w) in enumerate(regions):
         for a, (src, dst) in enumerate(((w_in, W), (d_in, D), (e_in, E), (n_in, N), (s_in, S))):
@@ -147,7 +152,7 @@
                     load_sem.at[k * 5 + a],
                 )
             )
-    loads.append(pltpu.make_async_copy(a_in, active, load_sem.at[25]))
+    loads.append(pltpu.make_async_copy(a_in, active, load_sem.at[5 * len(regions)]))
     for copy in loads:
         copy.start()
 
@@ -225,7 +230,7 @@
     def depth_of(r, h, t):
         return cell(D, r, h, t) * (0.5 * cell(W, r, h, t).astype(F32))
 
-    for copy in loads[:20]:
+    for copy in loads[:10]:
         copy.wait()
 
     lane = lanes_of((rows, LANES))
@@ -242,33 +247,55 @@
 
     pack_w[...] = pick(lane, [turn(sides[0][a], WIDE * a) for a in range(4)])
     pack_e[...] = pick(lane, [turn(sides[far][a], WIDE * (a + 1)) for a in range(4)])
+    pl.semaphore_wait(barrier, count)
+    start(halos[2:])
+
+    for copy in loads[10:20]:
+        copy.wait()
     for a, f in enumerate((S, E, N, None)):
         for t in range(tiles):
             for buffer, to, r in ((TOP, HALO, 0), (BOT, 0, rows - edge)):
                 v = depth_of(r, edge, t) if f is None else cell(f, r, edge, t)
                 buffer[a, to : to + edge, span(t)] = v
 
-    pl.semaphore_wait(barrier, count)
-    start(halos)
+    start(halos[:2])
 
     for a in range(4):
         Z[a] = jnp.where(lane < 64, turn(sides[far][a], WIDE), turn(sides[0][a], -WIDE))
 
-    for copy in loads[20:]:
-        copy.wait()
-
-    def read(f):
-        return [cell(f, 0, rows, t) for t in range(tiles)]
-
-    def write(f, x):
+    def read(f, r=0, h=rows):
+        return [cell(f, r, h, t) for t in range(tiles)]
+
+    def write(f, x, r=0):
         for t, v in enumerate(x):
-            f[:, span(t)] = v
-
-    m = [0.5 * v.astype(F32) for v in read(W)]
-    depth = [v * w for v, w in zip(read(D), m)]
-    s, e, n, cx, cy = first_step(read(S), read(E), read(N), depth, m)
-    for f, x in ((S, s), (E, e), (N, n), (D, cx), (CY, cy), (M, m)):
-        write(f, x)
+            f[r : r + v.shape[0], span(t)] = v
+
+    n_before = None
+    begin = 0
+    for k, (r, h) in enumerate(chunks):
+        for copy in loads[20 + 5 * k : 25 + 5 * k]:
+            copy.wait()
+        last = k == len(chunks) - 1
+        end = rows if last else r + h - HALO
+        height = end - begin
+        m = [0.5 * v.astype(F32) for v in read(W, begin, height)]
+        depth = [v * w for v, w in zip(read(D, begin, height), m)]
+        after = (None, None, None)
+        if not last:
+            half = [0.5 * v.astype(F32) for v in read(W, end, HALO)]
+            after = (
+                read(S, end, HALO),
+                [v * (w + w) for v, w in zip(read(N, end, HALO), half)],
+                [v * w for v, w in zip(read(D, end, HALO), half)],
+            )
+        s, e, n, cx, cy = first_step(
+            read(S, begin, height), read(E, begin, height), read(N, begin, height), depth, m, after, n_before
+        )
+        for f, x in ((S, s), (E, e), (N, n), (D, cx), (CY, cy), (M, m)):
+            write(f, x, begin)
+        n_before = [v[height - HALO :] for v in n]
+        begin = end
+    loads[-1].wait()
 
     for step in range(STEPS - 2):
         s, e, n = next_step(*(read(f) for f in (S, E, N, D, CY, M)))
@@ -339,6 +366,40 @@
         fields.append([pick(lane, pieces)])
     strip = march(*fields)
 
+    row_sums(strip[0][0], tiles)
+    cells = rows // SPACING
+
+    def beyond(x):
+        at = lanes_of(x.shape)
+        x = jnp.where(at < 64, turn(x, WIDE), turn(x, -WIDE))
+        return jnp.where((at >= WIDE) & (at < 3 * WIDE), x, 0.0)
+
+    for t in range(tiles + 1):
+        south, north = edges[0][0][t][HALO:edge], edges[1][0][t][HALO:edge]
+        if t == tiles:
+            south, north = beyond(south), beyond(north)
+        for k in range(4):
+            R[k : k + 1, span(t)] += total_of(south * lower[k])
+            R[cells + k : cells + k + 1, span(t)] += total_of(north * upper[k])
+
+    points = R.shape[0]
+
+    def dot(x, w):
+        return jnp.dot(x, w, precision=lax.Precision.HIGHEST, preferred_element_type=F32)
+
+    spread = dot(jnp.concatenate([R[:, span(t)] for t in range(tiles)], axis=0), column_weight)
+    own = dot(R[:, span(tiles)], strip_weight)
+    for t in range(tiles):
+        own = own + turn(spread[t * points : (t + 1) * points], 8 * t)
+    PART[...] = own
+
+    top, bottom = pl.ds(0, HALO), pl.ds(points - HALO, HALO)
+    cross = messages([
+        (PART.at[bottom], fold.at[0], NORTH),
+        (PART.at[top], fold.at[1], SOUTH),
+    ], len(halos))
+    start(cross)
+
     middle = slice(HALO, rows - HALO)
     for f, z, south, north in zip((s_out, e_out, n_out), strip, *edges):
         x = lanes_of((rows - 2 * HALO, LANES))
@@ -348,39 +409,6 @@
             f[0:HALO, span(t)] = south[t][HALO:edge]
             f[rows - HALO : rows, span(t)] = north[t][HALO:edge]
 
-    row_sums(strip[0][0], tiles)
-    cells = rows // SPACING
-
-    def beyond(x):
-        at = lanes_of(x.shape)
-        x = jnp.where(at < 64, turn(x, WIDE), turn(x, -WIDE))
-        return jnp.where((at >= WIDE) & (at < 3 * WIDE), x, 0.0)
-
-    for t in range(tiles + 1):
-        south, north = edges[0][0][t][HALO:edge], edges[1][0][t][HALO:edge]
-        if t == tiles:
-            south, north = beyond(south), beyond(north)
-        for k in range(4):
-            R[k : k + 1, span(t)] += total_of(south * lower[k])
-            R[cells + k : cells + k + 1, span(t)] += total_of(north * upper[k])
-
-    points = R.shape[0]
-
-    def dot(x, w):
-        return jnp.dot(x, w, precision=lax.Precision.HIGHEST, preferred_element_type=F32)
-
-    spread = dot(jnp.concatenate([R[:, span(t)] for t in range(tiles)], axis=0), column_weight)
-    own = dot(R[:, span(tiles)], strip_weight)
-    for t in range(tiles):
-        own = own + turn(spread[t * points : (t + 1) * points], 8 * t)
-    PART[...] = own
-
-    top, bottom = pl.ds(0, HALO), pl.ds(points - HALO, HALO)
-    cross = messages([
-        (PART.at[bottom], fold.at[0], NORTH),
-        (PART.at[top], fold.at[1], SOUTH),
-    ], len(halos))
-    start(cross)
     finish(cross)
 
     row = lax.broadcasted_iota(jnp.int32, (HALO, LANES), 0)
@@ -395,7 +423,15 @@
 
 def deliver(*refs):
     sem = refs[8]
-    copies = [pltpu.make_async_copy(refs[k], refs[4 + k], sem.at[k]) for k in range(4)]
+    copies = []
+    for k in range(3):
+        rows = refs[k].shape[0] // PIECES
+        for p in range(PIECES):
+            here = pl.ds(p * rows, rows)
+            copies.append(
+                pltpu.make_async_copy(refs[k].at[here], refs[4 + k].at[here], sem.at[len(copies)])
+            )
+    copies.append(pltpu.make_async_copy(refs[3], refs[7], sem.at[len(copies)]))
     for copy in copies:
         copy.start()
     for copy in copies:
@@ -430,7 +466,7 @@
             pack, pack, pack, pack,
             pltpu.VMEM((4, HALO, LANES), F32),
             pltpu.VMEM((2, HALO, LANES), F32),
-            pltpu.SemaphoreType.DMA((26,)),
+            pltpu.SemaphoreType.DMA((5 * (4 + CHUNKS) + 1,)),
             pltpu.SemaphoreType.DMA((10,)),
             pltpu.SemaphoreType.DMA((10,)),
         ],
@@ -443,7 +479,7 @@
         out_shape=(shape, shape, shape, jax.ShapeDtypeStruct(control_active.shape, F32)),
         in_specs=[whole] * 4,
         out_specs=(in_hbm,) * 4,
-        scratch_shapes=[pltpu.SemaphoreType.DMA((4,))],
+        scratch_shapes=[pltpu.SemaphoreType.DMA((3 * PIECES + 1,))],
     )(*[pltpu.with_memory_space_constraint(x, pltpu.VMEM) for x in (s, e, n, g)])
 
 

time: 20.3 us -> 20.3 us (level)
  no operation moved by 1% of the time
where the time goes in v5:
time: 20.3 us
  Pallas kernels  19.6 us (97%)
  between operations  0.64 us (3%)
    pallas_call x1, Pallas kernels, local(): pl.pallas_call(kernel, out_shape=(shape, shape, shape, jax.ShapeDtypeStru...  17.9 us
    pallas_call x1, Pallas kernels, local(): pl.pallas_call(deliver, out_shape=(shape, shape, shape, jax.ShapeDtypeStr...  1.7 us

profile of v5, /device:TPU:25, one launch (start us, length us, event | category | flops | bytes accessed | tf_op | source)
XLA Modules:
  0.0 20.3 jit_solution(1185394482935941702)
XLA Ops:
  0.6 17.9 %shard_map.93 = (f32[256,1024]{1,0:T(8,128)S(1)}, f32[256,1024]{1,0:T(8,128)S(1)}, f32[256,1024]{1,0:T(8,128)S(1)}, f32[16,64]{1,0:T(8,128)S(1)}) custom-call(f32[256,1024]{1,0:T(8,128)} %s_in.1, f32[256,1024]{1,0:T(8,128)} %e_in.1, f32[256,1024]{1,0:T(8,128)} %n_in.1, f32[256,1024]{1,0:T(8,128)} %d_in.1, s32[256,1024]{1,0:T(8,128)} %w_in.1, s32[16,64]{1,0:T(8,128)} %a_in.1), custom_call_target="tpu_custom_call" | custom-call | tf_op jit(solution)/shard_map/pallas_call | solution.py:452
  18.6 1.7 %shard_map.94 = (f32[256,1024]{1,0:T(8,128)}, f32[256,1024]{1,0:T(8,128)}, f32[256,1024]{1,0:T(8,128)}, f32[16,64]{1,0:T(8,128)}) custom-call(f32[256,1024]{1,0:T(8,128)S(1)} %get-tuple-element.8.refs_0_, f32[256,1024]{1,0:T(8,128)S(1)} %get-tuple-element.9.refs_1_, f32[256,1024]{1,0:T(8,128)S(1)} %get-tuple-element.10.refs_2_, ...), custom_call_target="tpu_custom_call" | custom-call | tf_op jit(solution)/shard_map/pallas_call | solution.py:477

commit v6 on v5

--- a/solution.py
+++ b/solution.py
@@ -313,24 +313,30 @@
     def total_of(x):
         return jnp.sum(x, axis=0, keepdims=True)
 
-    def row_sums(v, t):
+    cells = rows // SPACING
+
+    def row_sums(v, t, whole):
         none = jnp.zeros((HALO, LANES), F32)
         c = [none] * 4
-        cells = rows // SPACING
         for q in range(cells):
             r = q * SPACING
             low, high = v[r : r + HALO], v[r + HALO : r + SPACING]
-            a = [none] * 4 if q == 0 else [low * w for w in lower]
-            b = [none] * 4 if q == cells - 1 else [high * w for w in upper]
+            a = [low * w for w in lower] if whole or q > 0 else [none] * 4
+            b = [high * w for w in upper] if whole or q < cells - 1 else [none] * 4
             R[q : q + 1, span(t)] = total_of(c[0] + a[0])
             c = [c[1] + (a[1] + b[0]), c[2] + (a[2] + b[1]), c[3] + (a[3] + b[2]), b[3]]
         for k in range(4):
             R[cells + k : cells + k + 1, span(t)] = total_of(c[k])
 
-    s[0] = jnp.where(lane >= 8, s[0], 0.0)
-    s[far] = jnp.where(lane < LANES - 8, s[far], 0.0)
+    def inner_columns(x):
+        at = lanes_of(x[0].shape)
+        x[0] = jnp.where(at >= 8, x[0], 0.0)
+        x[far] = jnp.where(at < LANES - 8, x[far], 0.0)
+        return x
+
+    s = inner_columns(s)
     for t in range(tiles):
-        row_sums(s[t], t)
+        row_sums(s[t], t, False)
 
     shape = (LANES, LANES)
     at = lax.broadcasted_iota(jnp.int32, shape, 0)
@@ -340,57 +346,44 @@
     strip_weight = spline_weight((strip_column.astype(F32) + 0.5) / SPACING - point)
     strip_weight = jnp.where((at >= WIDE - 8) & (at < 3 * WIDE + 8), strip_weight, 0.0)
 
-    finish(halos)
-
-    def ring(east, west, a):
-        x = lanes_of(east.shape)
-        east, west = turn(east, -WIDE * a), turn(west, -WIDE * (a + 1))
-        return jnp.where(x < WIDE, east, jnp.where(x >= LANES - WIDE, west, 0.0))
-
-    edges = []
-    for buffer in (TOP, BOT):
-        fields = []
-        for a in range(4):
-            if buffer is TOP:
-                parts = [ring(corner[1], corner[0], a), ring(got_e[0:edge], got_w[0:edge], a)]
-            else:
-                last = slice(rows - edge, rows)
-                parts = [ring(got_e[last], got_w[last], a), ring(corner[3], corner[2], a)]
-            fields.append([buffer[a, :, span(t)] for t in range(tiles)] + [jnp.concatenate(parts, axis=0)])
-        edges.append(march(*fields))
-
+    def dot(x, w):
+        return jnp.dot(x, w, precision=lax.Precision.HIGHEST, preferred_element_type=F32)
+
+    finish(halos[:2])
+    edges = [march(*([buffer[a, :, span(t)] for t in range(tiles)] for a in range(4))) for buffer in (TOP, BOT)]
+    for f, south, north in zip((s_out, e_out, n_out), *edges):
+        for t in range(tiles):
+            f[0:HALO, span(t)] = south[t][HALO:edge]
+            f[rows - HALO : rows, span(t)] = north[t][HALO:edge]
+    south = inner_columns([v[HALO:edge] for v in edges[0][0]])
+    north = inner_columns([v[HALO:edge] for v in edges[1][0]])
+    for t in range(tiles):
+        for k in range(4):
+            R[k : k + 1, span(t)] += total_of(south[t] * lower[k])
+            R[cells + k : cells + k + 1, span(t)] += total_of(north[t] * upper[k])
+
+    points = R.shape[0]
+    spread = dot(jnp.concatenate([R[:, span(t)] for t in range(tiles)], axis=0), column_weight)
+    own = spread[0:points]
+    for t in range(1, tiles):
+        own = own + turn(spread[t * points : (t + 1) * points], 8 * t)
+
+    finish(halos[2:])
     fields = []
     for a in range(4):
-        own = Z[a]
-        pieces = [own, turn(got_e[...], WIDE * (1 - a)), turn(got_w[...], WIDE * (2 - a)), own]
-        fields.append([pick(lane, pieces)])
-    strip = march(*fields)
-
-    row_sums(strip[0][0], tiles)
-    cells = rows // SPACING
-
-    def beyond(x):
-        at = lanes_of(x.shape)
-        x = jnp.where(at < 64, turn(x, WIDE), turn(x, -WIDE))
-        return jnp.where((at >= WIDE) & (at < 3 * WIDE), x, 0.0)
-
-    for t in range(tiles + 1):
-        south, north = edges[0][0][t][HALO:edge], edges[1][0][t][HALO:edge]
-        if t == tiles:
-            south, north = beyond(south), beyond(north)
-        for k in range(4):
-            R[k : k + 1, span(t)] += total_of(south * lower[k])
-            R[cells + k : cells + k + 1, span(t)] += total_of(north * upper[k])
-
-    points = R.shape[0]
-
-    def dot(x, w):
-        return jnp.dot(x, w, precision=lax.Precision.HIGHEST, preferred_element_type=F32)
-
-    spread = dot(jnp.concatenate([R[:, span(t)] for t in range(tiles)], axis=0), column_weight)
-    own = dot(R[:, span(tiles)], strip_weight)
-    for t in range(tiles):
-        own = own + turn(spread[t * points : (t + 1) * points], 8 * t)
+        parts = []
+        for near, east, west in (
+            ([TOP[a, 0:HALO, span(t)] for t in (far, 0)], corner[1], corner[0]),
+            (None, got_e[...], got_w[...]),
+            ([BOT[a, edge : edge + HALO, span(t)] for t in (far, 0)], corner[3], corner[2]),
+        ):
+            x = lanes_of(east.shape)
+            mine = Z[a] if near is None else jnp.where(x < 64, turn(near[0], WIDE), turn(near[1], -WIDE))
+            parts.append(pick(x, [mine, turn(east, WIDE * (1 - a)), turn(west, WIDE * (2 - a)), mine]))
+        fields.append([jnp.concatenate(parts, axis=0)])
+    strip = [x[0][HALO : HALO + rows] for x in march(*fields)]
+    row_sums(strip[0], tiles, True)
+    own = own + dot(R[:, span(tiles)], strip_weight)
     PART[...] = own
 
     top, bottom = pl.ds(0, HALO), pl.ds(points - HALO, HALO)
@@ -400,15 +393,9 @@
     ], len(halos))
     start(cross)
 
-    middle = slice(HALO, rows - HALO)
-    for f, z, south, north in zip((s_out, e_out, n_out), strip, *edges):
-        x = lanes_of((rows - 2 * HALO, LANES))
-        f[middle, span(0)] = jnp.where(x < 8, turn(z[0][middle], WIDE), f[middle, span(0)])
-        f[middle, span(far)] = jnp.where(x >= LANES - 8, turn(z[0][middle], -WIDE), f[middle, span(far)])
-        for t in range(tiles):
-            f[0:HALO, span(t)] = south[t][HALO:edge]
-            f[rows - HALO : rows, span(t)] = north[t][HALO:edge]
-
+    for f, z in zip((s_out, e_out, n_out), strip):
+        f[:, span(0)] = jnp.where(lane < 8, turn(z, WIDE), f[:, span(0)])
+        f[:, span(far)] = jnp.where(lane >= LANES - 8, turn(z, -WIDE), f[:, span(far)])
     finish(cross)
 
     row = lax.broadcasted_iota(jnp.int32, (HALO, LANES), 0)

time: 20.3 us -> 19.6 us (0.966)
  Pallas kernels: 19.6 us -> 18.9 us
    pallas_call x1, Pallas kernels: 17.9 us -> 17.2 us  [local(): pl.pallas_call(kernel, out_shape=(shape, shape, shape, jax.ShapeDtypeStru...]
where the time goes in v6:
time: 19.6 us; the launch traced here: 19.5 us
  Pallas kernels  18.9 us (96%)
  between operations  0.64 us (3%)
    pallas_call x1, Pallas kernels, local(): pl.pallas_call(kernel, out_shape=(shape, shape, shape, jax.ShapeDtypeStru...  17.2 us
    pallas_call x1, Pallas kernels, local(): pl.pallas_call(deliver, out_shape=(shape, shape, shape, jax.ShapeDtypeStr...  1.7 us

profile of v6, /device:TPU:25, one launch (start us, length us, event | category | flops | bytes accessed | tf_op | source)
XLA Modules:
  0.0 19.5 jit_solution(16916218994941844252)
XLA Ops:
  0.6 17.2 %shard_map.93 = (f32[256,1024]{1,0:T(8,128)S(1)}, f32[256,1024]{1,0:T(8,128)S(1)}, f32[256,1024]{1,0:T(8,128)S(1)}, f32[16,64]{1,0:T(8,128)S(1)}) custom-call(f32[256,1024]{1,0:T(8,128)} %s_in.1, f32[256,1024]{1,0:T(8,128)} %e_in.1, f32[256,1024]{1,0:T(8,128)} %n_in.1, f32[256,1024]{1,0:T(8,128)} %d_in.1, s32[256,1024]{1,0:T(8,128)} %w_in.1, s32[16,64]{1,0:T(8,128)} %a_in.1), custom_call_target="tpu_custom_call" | custom-call | tf_op jit(solution)/shard_map/pallas_call | solution.py:439
  17.8 1.7 %shard_map.94 = (f32[256,1024]{1,0:T(8,128)}, f32[256,1024]{1,0:T(8,128)}, f32[256,1024]{1,0:T(8,128)}, f32[16,64]{1,0:T(8,128)}) custom-call(f32[256,1024]{1,0:T(8,128)S(1)} %get-tuple-element.8.refs_0_, f32[256,1024]{1,0:T(8,128)S(1)} %get-tuple-element.9.refs_1_, f32[256,1024]{1,0:T(8,128)S(1)} %get-tuple-element.10.refs_2_, ...), custom_call_target="tpu_custom_call" | custom-call | tf_op jit(solution)/shard_map/pallas_call | solution.py:464

commit v7 on v6

--- a/solution.py
+++ b/solution.py
@@ -104,7 +104,7 @@
     s_in, e_in, n_in, d_in, w_in, a_in,
     s_out, e_out, n_out, grad,
     S, E, N, D, W, CY, M, R, PART, active,
-    TOP, BOT, Z, pack_w, pack_e, got_w, got_e, corner, fold,
+    TOP, BOT, Z, pack_w, pack_e, got_w, got_e, corner, side, fold, RE,
     load_sem, send_sem, recv_sem,
 ):
     rows, cols = s_out.shape
@@ -188,25 +188,32 @@
 
     every = pl.ds(0, 4)
     body = pl.ds(0, cols)
+    first, final = pl.ds(0, WIDE), pl.ds(rows - WIDE, WIDE)
     halos = messages([
-        (TOP.at[every, pl.ds(HALO, HALO), body], BOT.at[every, pl.ds(edge, HALO), body], SOUTH),
-        (BOT.at[every, pl.ds(HALO, HALO), body], TOP.at[every, pl.ds(0, HALO), body], NORTH),
+        (TOP.at[every, pl.ds(edge, edge), body], BOT.at[every, pl.ds(edge, edge), body], SOUTH),
+        (BOT.at[every, pl.ds(0, edge), body], TOP.at[every, pl.ds(0, edge), body], NORTH),
         (pack_w, got_e, WEST),
         (pack_e, got_w, EAST),
-        (pack_w.at[pl.ds(0, HALO)], corner.at[3], SW),
-        (pack_e.at[pl.ds(0, HALO)], corner.at[2], SE),
-        (pack_w.at[pl.ds(rows - HALO, HALO)], corner.at[1], NW),
-        (pack_e.at[pl.ds(rows - HALO, HALO)], corner.at[0], NE),
+        (pack_w.at[first], corner.at[3], SW),
+        (pack_e.at[first], corner.at[2], SE),
+        (pack_w.at[final], corner.at[1], NW),
+        (pack_e.at[final], corner.at[0], NE),
+        (pack_w.at[first], side.at[2], SOUTH),
+        (pack_e.at[first], side.at[3], SOUTH),
+        (pack_w.at[final], side.at[0], NORTH),
+        (pack_e.at[final], side.at[1], NORTH),
     ], 0)
 
     @pl.when(lat == 0)
     def _():
-        TOP[:, 0:HALO, 0:cols] = jnp.zeros((4, HALO, cols), F32)
+        TOP[:, 0:edge, 0:cols] = jnp.zeros((4, edge, cols), F32)
+        side[0:2] = jnp.zeros_like(side[0:2])
         fold[0] = jnp.zeros_like(fold[0])
 
     @pl.when(lat == nlat - 1)
     def _():
-        BOT[:, edge : edge + HALO, 0:cols] = jnp.zeros((4, HALO, cols), F32)
+        BOT[:, edge : 2 * edge, 0:cols] = jnp.zeros((4, edge, cols), F32)
+        side[2:4] = jnp.zeros_like(side[2:4])
         fold[1] = jnp.zeros_like(fold[1])
 
     for pack, offset in ((got_w, WEST), (got_e, EAST)):
@@ -254,7 +261,7 @@
         copy.wait()
     for a, f in enumerate((S, E, N, None)):
         for t in range(tiles):
-            for buffer, to, r in ((TOP, HALO, 0), (BOT, 0, rows - edge)):
+            for buffer, to, r in ((TOP, edge, 0), (BOT, 0, rows - edge)):
                 v = depth_of(r, edge, t) if f is None else cell(f, r, edge, t)
                 buffer[a, to : to + edge, span(t)] = v
 
@@ -315,18 +322,30 @@
 
     cells = rows // SPACING
 
-    def row_sums(v, t, whole):
+    def row_sums(v, t):
         none = jnp.zeros((HALO, LANES), F32)
         c = [none] * 4
         for q in range(cells):
             r = q * SPACING
             low, high = v[r : r + HALO], v[r + HALO : r + SPACING]
-            a = [low * w for w in lower] if whole or q > 0 else [none] * 4
-            b = [high * w for w in upper] if whole or q < cells - 1 else [none] * 4
+            a = [low * w for w in lower] if q > 0 else [none] * 4
+            b = [high * w for w in upper] if q < cells - 1 else [none] * 4
             R[q : q + 1, span(t)] = total_of(c[0] + a[0])
             c = [c[1] + (a[1] + b[0]), c[2] + (a[2] + b[1]), c[3] + (a[3] + b[2]), b[3]]
         for k in range(4):
             R[cells + k : cells + k + 1, span(t)] = total_of(c[k])
+
+    def strip_sums(v):
+        none = jnp.zeros((HALO, LANES), F32)
+        c = [none] * 4
+        for q in range(-2, cells + 2):
+            r = WIDE + q * SPACING
+            low, high = v[r : r + HALO], v[r + HALO : r + SPACING]
+            a = [low * w for w in lower] if q > -2 else [none] * 4
+            b = [high * w for w in upper] if q < cells + 1 else [none] * 4
+            if q >= 2:
+                R[q : q + 1, span(tiles)] = total_of(c[0] + a[0])
+            c = [c[1] + (a[1] + b[0]), c[2] + (a[2] + b[1]), c[3] + (a[3] + b[2]), b[3]]
 
     def inner_columns(x):
         at = lanes_of(x[0].shape)
@@ -336,7 +355,7 @@
 
     s = inner_columns(s)
     for t in range(tiles):
-        row_sums(s[t], t, False)
+        row_sums(s[t], t)
 
     shape = (LANES, LANES)
     at = lax.broadcasted_iota(jnp.int32, shape, 0)
@@ -349,49 +368,62 @@
     def dot(x, w):
         return jnp.dot(x, w, precision=lax.Precision.HIGHEST, preferred_element_type=F32)
 
-    finish(halos[:2])
-    edges = [march(*([buffer[a, :, span(t)] for t in range(tiles)] for a in range(4))) for buffer in (TOP, BOT)]
-    for f, south, north in zip((s_out, e_out, n_out), *edges):
-        for t in range(tiles):
-            f[0:HALO, span(t)] = south[t][HALO:edge]
-            f[rows - HALO : rows, span(t)] = north[t][HALO:edge]
-    south = inner_columns([v[HALO:edge] for v in edges[0][0]])
-    north = inner_columns([v[HALO:edge] for v in edges[1][0]])
-    for t in range(tiles):
-        for k in range(4):
-            R[k : k + 1, span(t)] += total_of(south[t] * lower[k])
-            R[cells + k : cells + k + 1, span(t)] += total_of(north[t] * upper[k])
+    def along(f):
+        h = f.shape[0]
+        spread = dot(jnp.concatenate([f[:, span(t)] for t in range(tiles)], axis=0), column_weight)
+        total = spread[0:h]
+        for t in range(1, tiles):
+            total = total + turn(spread[t * h : (t + 1) * h], 8 * t)
+        return total
 
     points = R.shape[0]
-    spread = dot(jnp.concatenate([R[:, span(t)] for t in range(tiles)], axis=0), column_weight)
-    own = spread[0:points]
-    for t in range(1, tiles):
-        own = own + turn(spread[t * points : (t + 1) * points], 8 * t)
-
-    finish(halos[2:])
-    fields = []
-    for a in range(4):
-        parts = []
-        for near, east, west in (
-            ([TOP[a, 0:HALO, span(t)] for t in (far, 0)], corner[1], corner[0]),
-            (None, got_e[...], got_w[...]),
-            ([BOT[a, edge : edge + HALO, span(t)] for t in (far, 0)], corner[3], corner[2]),
-        ):
-            x = lanes_of(east.shape)
-            mine = Z[a] if near is None else jnp.where(x < 64, turn(near[0], WIDE), turn(near[1], -WIDE))
-            parts.append(pick(x, [mine, turn(east, WIDE * (1 - a)), turn(west, WIDE * (2 - a)), mine]))
-        fields.append([jnp.concatenate(parts, axis=0)])
-    strip = [x[0][HALO : HALO + rows] for x in march(*fields)]
-    row_sums(strip[0], tiles, True)
-    own = own + dot(R[:, span(tiles)], strip_weight)
+    own = along(R)
     PART[...] = own
-
     top, bottom = pl.ds(0, HALO), pl.ds(points - HALO, HALO)
     cross = messages([
         (PART.at[bottom], fold.at[0], NORTH),
         (PART.at[top], fold.at[1], SOUTH),
     ], len(halos))
     start(cross)
+
+    finish(halos[:2])
+    edges = [march(*([buffer[a, :, span(t)] for t in range(tiles)] for a in range(4))) for buffer in (TOP, BOT)]
+    for f, south, north in zip((s_out, e_out, n_out), *edges):
+        for t in range(tiles):
+            f[0:HALO, span(t)] = south[t][edge : edge + HALO]
+            f[rows - HALO : rows, span(t)] = north[t][HALO:edge]
+    south = inner_columns([v[HALO : edge + HALO] for v in edges[0][0]])
+    north = inner_columns([v[HALO : edge + HALO] for v in edges[1][0]])
+    for t in range(tiles):
+        for k in range(4):
+            RE[k : k + 1, span(t)] = total_of(south[t][:HALO] * upper[k] + south[t][HALO:] * lower[k])
+            RE[4 + k : 5 + k, span(t)] = total_of(north[t][:HALO] * upper[k] + north[t][HALO:] * lower[k])
+    more = along(RE)
+    none = jnp.zeros((4, LANES), F32)
+    own = jnp.concatenate([
+        own[:HALO] + jnp.concatenate([more[0:4], none], axis=0),
+        own[HALO : points - HALO],
+        own[points - HALO :] + jnp.concatenate([more[4:8], none], axis=0),
+    ], axis=0)
+
+    finish(halos[2:])
+    fields = []
+    for a in range(4):
+        parts = []
+        for last, east, west, near in (
+            (side[1], corner[1], corner[0], side[0]),
+            (None, got_e[...], got_w[...], None),
+            (side[3], corner[3], corner[2], side[2]),
+        ):
+            x = lanes_of(east.shape)
+            last = Z[a] if last is None else turn(last, -WIDE * a)
+            near = Z[a] if near is None else turn(near, WIDE * (3 - a))
+            parts.append(pick(x, [last, turn(east, WIDE * (1 - a)), turn(west, WIDE * (2 - a)), near]))
+        fields.append([jnp.concatenate(parts, axis=0)])
+    strip = [x[0] for x in march(*fields)]
+    strip_sums(strip[0])
+    strip = [x[WIDE : WIDE + rows] for x in strip]
+    own = own + dot(R[:, span(tiles)], strip_weight)
 
     for f, z in zip((s_out, e_out, n_out), strip):
         f[:, span(0)] = jnp.where(lane < 8, turn(z, WIDE), f[:, span(0)])
@@ -430,7 +462,7 @@
     points = rows // SPACING + 4
     points = (points + 7) // 8 * 8
     field = pltpu.VMEM((rows, cols), F32)
-    rim = pltpu.VMEM((4, 3 * HALO, cols), F32)
+    rim = pltpu.VMEM((4, 4 * HALO, cols), F32)
     pack = pltpu.VMEM((rows, LANES), F32)
     whole = pl.BlockSpec(memory_space=pltpu.VMEM)
     in_hbm = pl.BlockSpec(memory_space=pltpu.HBM)
@@ -451,11 +483,13 @@
             rim, rim,
             pltpu.VMEM((4, rows, LANES), F32),
             pack, pack, pack, pack,
-            pltpu.VMEM((4, HALO, LANES), F32),
+            pltpu.VMEM((4, WIDE, LANES), F32),
+            pltpu.VMEM((4, WIDE, LANES), F32),
             pltpu.VMEM((2, HALO, LANES), F32),
+            pltpu.VMEM((HALO, cols), F32),
             pltpu.SemaphoreType.DMA((5 * (4 + CHUNKS) + 1,)),
-            pltpu.SemaphoreType.DMA((10,)),
-            pltpu.SemaphoreType.DMA((10,)),
+            pltpu.SemaphoreType.DMA((14,)),
+            pltpu.SemaphoreType.DMA((14,)),
         ],
         compiler_params=pltpu.CompilerParams(
             collective_id=0, has_side_effects=True, vmem_limit_bytes=32 * 1024 * 1024

time: 19.6 us -> 18.2 us (0.929)
  Pallas kernels: 18.9 us -> 17.5 us
    pallas_call x1, Pallas kernels: 17.2 us -> 15.8 us  [local(): pl.pallas_call(kernel, out_shape=(shape, shape, shape, jax.ShapeDtypeStru...]
where the time goes in v7:
time: 18.2 us; the launch traced here: 18.1 us
  Pallas kernels  17.5 us (96%)
  between operations  0.64 us (4%)
    pallas_call x1, Pallas kernels, local(): pl.pallas_call(kernel, out_shape=(shape, shape, shape, jax.ShapeDtypeStru...  15.8 us
    pallas_call x1, Pallas kernels, local(): pl.pallas_call(deliver, out_shape=(shape, shape, shape, jax.ShapeDtypeStr...  1.7 us

profile of v7, /device:TPU:25, one launch (start us, length us, event | category | flops | bytes accessed | tf_op | source)
XLA Modules:
  0.0 18.1 jit_solution(5734267973082088345)
XLA Ops:
  0.6 15.8 %shard_map.93 = (f32[256,1024]{1,0:T(8,128)S(1)}, f32[256,1024]{1,0:T(8,128)S(1)}, f32[256,1024]{1,0:T(8,128)S(1)}, f32[16,64]{1,0:T(8,128)S(1)}) custom-call(f32[256,1024]{1,0:T(8,128)} %s_in.1, f32[256,1024]{1,0:T(8,128)} %e_in.1, f32[256,1024]{1,0:T(8,128)} %n_in.1, f32[256,1024]{1,0:T(8,128)} %d_in.1, s32[256,1024]{1,0:T(8,128)} %w_in.1, s32[16,64]{1,0:T(8,128)} %a_in.1), custom_call_target="tpu_custom_call" | custom-call | tf_op jit(solution)/shard_map/pallas_call | solution.py:471
  16.4 1.7 %shard_map.94 = (f32[256,1024]{1,0:T(8,128)}, f32[256,1024]{1,0:T(8,128)}, f32[256,1024]{1,0:T(8,128)}, f32[16,64]{1,0:T(8,128)}) custom-call(f32[256,1024]{1,0:T(8,128)S(1)} %get-tuple-element.8.refs_0_, f32[256,1024]{1,0:T(8,128)S(1)} %get-tuple-element.9.refs_1_, f32[256,1024]{1,0:T(8,128)S(1)} %get-tuple-element.10.refs_2_, ...), custom_call_target="tpu_custom_call" | custom-call | tf_op jit(solution)/shard_map/pallas_call | solution.py:498

commit v8 on v7

--- a/solution.py
+++ b/solution.py
@@ -253,7 +253,7 @@
         return total
 
     pack_w[...] = pick(lane, [turn(sides[0][a], WIDE * a) for a in range(4)])
-    pack_e[...] = pick(lane, [turn(sides[far][a], WIDE * (a + 1)) for a in range(4)])
+    pack_e[...] = pick(lane, [turn(sides[far][a], WIDE * (a - 2)) for a in (3, 0, 1, 2)])
     pl.semaphore_wait(barrier, count)
     start(halos[2:])
 
@@ -268,7 +268,7 @@
     start(halos[:2])
 
     for a in range(4):
-        Z[a] = jnp.where(lane < 64, turn(sides[far][a], WIDE), turn(sides[0][a], -WIDE))
+        Z[a] = jnp.where(lane < WIDE, sides[0][a], turn(sides[far][a], 2 * WIDE))
 
     def read(f, r=0, h=rows):
         return [cell(f, r, h, t) for t in range(tiles)]
@@ -361,9 +361,9 @@
     at = lax.broadcasted_iota(jnp.int32, shape, 0)
     point = lanes_of(shape).astype(F32) - 2.0 + 0.5
     column_weight = spline_weight((at.astype(F32) + 0.5) / SPACING - point)
-    strip_column = jnp.where(at < 64, at + (cols - WIDE), at - 3 * WIDE)
+    strip_column = jnp.where(at < WIDE, at, jnp.where(at < 3 * WIDE, at + (cols - 2 * WIDE), at - LANES))
     strip_weight = spline_weight((strip_column.astype(F32) + 0.5) / SPACING - point)
-    strip_weight = jnp.where((at >= WIDE - 8) & (at < 3 * WIDE + 8), strip_weight, 0.0)
+    strip_weight = jnp.where((at < 8) | (at >= 2 * WIDE - 8), strip_weight, 0.0)
 
     def dot(x, w):
         return jnp.dot(x, w, precision=lax.Precision.HIGHEST, preferred_element_type=F32)
@@ -416,9 +416,10 @@
             (side[3], corner[3], corner[2], side[2]),
         ):
             x = lanes_of(east.shape)
-            last = Z[a] if last is None else turn(last, -WIDE * a)
-            near = Z[a] if near is None else turn(near, WIDE * (3 - a))
-            parts.append(pick(x, [last, turn(east, WIDE * (1 - a)), turn(west, WIDE * (2 - a)), near]))
+            group = (x >= WIDE * a) & (x < WIDE * (a + 1))
+            mine = Z[a] if last is None else turn(jnp.where(group, near, last), -WIDE * a)
+            theirs = turn(jnp.where(group, east, west), WIDE * (2 - a))
+            parts.append(jnp.where(x < 2 * WIDE, mine, theirs))
         fields.append([jnp.concatenate(parts, axis=0)])
     strip = [x[0] for x in march(*fields)]
     strip_sums(strip[0])
@@ -426,8 +427,8 @@
     own = own + dot(R[:, span(tiles)], strip_weight)
 
     for f, z in zip((s_out, e_out, n_out), strip):
-        f[:, span(0)] = jnp.where(lane < 8, turn(z, WIDE), f[:, span(0)])
-        f[:, span(far)] = jnp.where(lane >= LANES - 8, turn(z, -WIDE), f[:, span(far)])
+        f[:, span(0)] = jnp.where(lane < 8, z, f[:, span(0)])
+        f[:, span(far)] = jnp.where(lane >= LANES - 8, turn(z, 2 * WIDE), f[:, span(far)])
     finish(cross)
 
     row = lax.broadcasted_iota(jnp.int32, (HALO, LANES), 0)

time: 18.2 us -> 18 us (0.989)
  Pallas kernels: 17.5 us -> 17.2 us
    pallas_call x1, Pallas kernels: 15.8 us -> 15.5 us  [local(): pl.pallas_call(kernel, out_shape=(shape, shape, shape, jax.ShapeDtypeStru...]
where the time goes in v8:
time: 18 us; the launch traced here: 17.8 us
  Pallas kernels  17.2 us (96%)
  between operations  0.64 us (4%)
    pallas_call x1, Pallas kernels, local(): pl.pallas_call(kernel, out_shape=(shape, shape, shape, jax.ShapeDtypeStru...  15.5 us
    pallas_call x1, Pallas kernels, local(): pl.pallas_call(deliver, out_shape=(shape, shape, shape, jax.ShapeDtypeStr...  1.7 us

profile of v8, /device:TPU:25, one launch (start us, length us, event | category | flops | bytes accessed | tf_op | source)
XLA Modules:
  0.0 17.8 jit_solution(7153488312664368583)
XLA Ops:
  0.6 15.5 %shard_map.93 = (f32[256,1024]{1,0:T(8,128)S(1)}, f32[256,1024]{1,0:T(8,128)S(1)}, f32[256,1024]{1,0:T(8,128)S(1)}, f32[16,64]{1,0:T(8,128)S(1)}) custom-call(f32[256,1024]{1,0:T(8,128)} %s_in.1, f32[256,1024]{1,0:T(8,128)} %e_in.1, f32[256,1024]{1,0:T(8,128)} %n_in.1, f32[256,1024]{1,0:T(8,128)} %d_in.1, s32[256,1024]{1,0:T(8,128)} %w_in.1, s32[16,64]{1,0:T(8,128)} %a_in.1), custom_call_target="tpu_custom_call" | custom-call | tf_op jit(solution)/shard_map/pallas_call | solution.py:472
  16.1 1.7 %shard_map.94 = (f32[256,1024]{1,0:T(8,128)}, f32[256,1024]{1,0:T(8,128)}, f32[256,1024]{1,0:T(8,128)}, f32[16,64]{1,0:T(8,128)}) custom-call(f32[256,1024]{1,0:T(8,128)S(1)} %get-tuple-element.8.refs_0_, f32[256,1024]{1,0:T(8,128)S(1)} %get-tuple-element.9.refs_1_, f32[256,1024]{1,0:T(8,128)S(1)} %get-tuple-element.10.refs_2_, ...), custom_call_target="tpu_custom_call" | custom-call | tf_op jit(solution)/shard_map/pallas_call | solution.py:499

commit v9 on v8

--- a/solution.py
+++ b/solution.py
@@ -254,9 +254,6 @@
 
     pack_w[...] = pick(lane, [turn(sides[0][a], WIDE * a) for a in range(4)])
     pack_e[...] = pick(lane, [turn(sides[far][a], WIDE * (a - 2)) for a in (3, 0, 1, 2)])
-    pl.semaphore_wait(barrier, count)
-    start(halos[2:])
-
     for copy in loads[10:20]:
         copy.wait()
     for a, f in enumerate((S, E, N, None)):
@@ -265,8 +262,6 @@
                 v = depth_of(r, edge, t) if f is None else cell(f, r, edge, t)
                 buffer[a, to : to + edge, span(t)] = v
 
-    start(halos[:2])
-
     for a in range(4):
         Z[a] = jnp.where(lane < WIDE, sides[0][a], turn(sides[far][a], 2 * WIDE))
 
@@ -276,6 +271,10 @@
     def write(f, x, r=0):
         for t, v in enumerate(x):
             f[r : r + v.shape[0], span(t)] = v
+
+    pl.semaphore_wait(barrier, count)
+    start(halos[2:])
+    start(halos[:2])
 
     n_before = None
     begin = 0

time: 18 us -> 18 us (level)
  no operation moved by 1% of the time
where the time goes in v9:
time: 18 us; the launch traced here: 17.9 us
  Pallas kernels  17.2 us (96%)
  between operations  0.64 us (4%)
    pallas_call x1, Pallas kernels, local(): pl.pallas_call(kernel, out_shape=(shape, shape, shape, jax.ShapeDtypeStru...  15.5 us
    pallas_call x1, Pallas kernels, local(): pl.pallas_call(deliver, out_shape=(shape, shape, shape, jax.ShapeDtypeStr...  1.7 us

profile of v9, /device:TPU:25, one launch (start us, length us, event | category | flops | bytes accessed | tf_op | source)
XLA Modules:
  0.0 17.9 jit_solution(16244924240639223757)
XLA Ops:
  0.6 15.5 %shard_map.93 = (f32[256,1024]{1,0:T(8,128)S(1)}, f32[256,1024]{1,0:T(8,128)S(1)}, f32[256,1024]{1,0:T(8,128)S(1)}, f32[16,64]{1,0:T(8,128)S(1)}) custom-call(f32[256,1024]{1,0:T(8,128)} %s_in.1, f32[256,1024]{1,0:T(8,128)} %e_in.1, f32[256,1024]{1,0:T(8,128)} %n_in.1, f32[256,1024]{1,0:T(8,128)} %d_in.1, s32[256,1024]{1,0:T(8,128)} %w_in.1, s32[16,64]{1,0:T(8,128)} %a_in.1), custom_call_target="tpu_custom_call" | custom-call | tf_op jit(solution)/shard_map/pallas_call | solution.py:471
  16.2 1.7 %shard_map.94 = (f32[256,1024]{1,0:T(8,128)}, f32[256,1024]{1,0:T(8,128)}, f32[256,1024]{1,0:T(8,128)}, f32[16,64]{1,0:T(8,128)}) custom-call(f32[256,1024]{1,0:T(8,128)S(1)} %get-tuple-element.8.refs_0_, f32[256,1024]{1,0:T(8,128)S(1)} %get-tuple-element.9.refs_1_, f32[256,1024]{1,0:T(8,128)S(1)} %get-tuple-element.10.refs_2_, ...), custom_call_target="tpu_custom_call" | custom-call | tf_op jit(solution)/shard_map/pallas_call | solution.py:498
